TPU v7x, 32 devices: a whole 2x2x4 slice. The times are simulated.
32 devices in a mesh: gx: 4 (over y, x), gy: 4 (over z), gz: 2 (over core).
Axes of the slice: x: 2, y: 2, z: 4, core: 2. Of those that a mesh axis runs over, the one named last changes fastest.
Arguments:
- tile_coords: int32 [3, 512], P(None, ('gx', 'gy', 'gz')), may hold values from 0 to 15, as said below
- owner_map: int32 [512], replicated, may hold values from 0 to 511, as said below
- bin_tile: int32 [1856], P(('gx', 'gy', 'gz')), may hold values from 0 to 511, as said below
- bin_count: int32 [1856], P(('gx', 'gy', 'gz')), may hold values from 0 to 2048, as said below
- part_cell: int32 [1856, 2048], P(('gx', 'gy', 'gz')), may hold values from 0 to 511
- part_offset: float32 [1856, 3, 2048], P(('gx', 'gy', 'gz')), may hold values from -0.5 to 0.5
- part_velocity: float32 [1856, 3, 2048], P(('gx', 'gy', 'gz')), may hold values from -5 to 5
- part_affine: float32 [1856, 9, 2048], P(('gx', 'gy', 'gz')), may hold values from -5 to 5
- part_mass: float32 [1856, 2048], P(('gx', 'gy', 'gz')), may hold values from 0.5 to 2
Outputs:
- grid_velocity: float32 [3, 262144], P(None, ('gx', 'gy', 'gz'))
- pressure: float32 [262144], P(('gx', 'gy', 'gz'))
- particle_velocity: float32 [1856, 3, 2048], P(('gx', 'gy', 'gz'))
Inputs may be any that keep to these rules, and one draw needn't show every extreme that they name: `tile_coords`: storage slot s lies on device s // 16 (device index over gx, gy, gz, slowest first). Coordinates are distinct; an active tile that shares a face with a tile stored on a device is stored on the same device or on one whose index differs by one along one mesh axis. `owner_map`: A permutation of the storage slots. `bin_tile`: the 58 bins of a device are first 32 bins whose tiles it stores itself, then 1 bins for each of the 26 offsets (dx, dy, dz) in -1..1 other than (0, 0, 0), in the order dx slowest, dz fastest, whose tiles are stored on the device at that offset of mesh indices. Bins of an offset that leads outside the mesh name some tile and hold no particles. The first bin_count slots of a bin hold its particles. Every device has a bin holding 2048.
All inputs are finite; a program needn't handle non-finite values.
Results may differ from a plain program's by a relative error of at most 0.0024.
The roundings to bfloat16 on the way count: a program that leaves them out, or rounds other values in their place, can miss the bound.
Values sent between devices are 32-bit elements; how exact they have to be, the bound alone decides.
A program may use at most 128 MiB of HBM per device.

v0:
```python
import jax
import jax.numpy as jnp
from jax import lax
from jax.sharding import PartitionSpec as P

TILE = 8
TPD = 16
SELF_BINS = 32
NBR_BINS = 1
SWEEPS = 4


gravity_step = 0.5
face_steps = [(1, 0, 0), (-1, 0, 0), (0, 1, 0), (0, -1, 0), (0, 0, 1), (0, 0, -1)]
neighbour_steps = [
    (along_x, along_y, along_z)
    for along_x in (-1, 0, 1)
    for along_y in (-1, 0, 1)
    for along_z in (-1, 0, 1)
    if (along_x, along_y, along_z) != (0, 0, 0)
]


def from_behind(block, axis, distance):
    devices = range(lax.axis_size(axis))
    route = [(i - distance, i) for i in devices if i - distance in devices]
    return lax.ppermute(block, axis, route)


def with_halo(block, sides, width):
    for axis, dim in sides:
        count = lax.axis_size(axis)
        forward = [(i, i + 1) for i in range(count - 1)]
        backward = [(target, source) for source, target in forward]
        low = lax.ppermute(
            lax.slice_in_dim(block, block.shape[dim] - width, None, axis=dim), axis, forward
        )
        high = lax.ppermute(lax.slice_in_dim(block, 0, width, axis=dim), axis, backward)
        block = jnp.concatenate([low, block, high], axis=dim)
    return block


def deposits(offsets, velocity, affine, masses, living):
    moments = []
    for component in range(3):
        drift_part = velocity[:, component] - (
            affine[:, 3 * component] * offsets[:, 0]
            + affine[:, 3 * component + 1] * offsets[:, 1]
            + affine[:, 3 * component + 2] * offsets[:, 2]
        )
        moments.append(masses * drift_part)
    stacked = jnp.stack([masses] + moments, axis=1)
    return jnp.where(living[:, None, :], stacked, 0.0).astype(jnp.bfloat16)


def group_of(count_bins):
    return [divisor for divisor in range(1, 9) if count_bins % divisor == 0][-1]


def splat_bins(amounts, upper_index, lower_index):
    count_bins = amounts.shape[0]
    capacity = amounts.shape[2]
    group_size = group_of(count_bins)
    plane_cells = TILE * TILE
    value_type = amounts.dtype

    def splat_block(pieces):
        amount_block, upper_block, lower_block = pieces
        upper_hot = (
            upper_block[:, None, :] == lax.broadcasted_iota(jnp.int32, (1, TILE, 1), 1)
        ).astype(value_type)
        weighted = (amount_block[:, :, None, :] * upper_hot[:, None, :, :]).reshape(
            group_size, 4 * TILE, capacity
        )
        lower_hot = (
            lower_block[:, :, None] == lax.broadcasted_iota(jnp.int32, (1, 1, plane_cells), 2)
        ).astype(value_type)
        summed = jnp.einsum(
            "gap,gpl->gal",
            weighted,
            lower_hot,
            precision=lax.Precision.HIGHEST,
            preferred_element_type=jnp.float32,
        )
        return summed.reshape(group_size, 4, TILE * plane_cells)

    blocks = lax.map(
        splat_block,
        (
            amounts.reshape(count_bins // group_size, group_size, 4, capacity),
            upper_index.reshape(count_bins // group_size, group_size, capacity),
            lower_index.reshape(count_bins // group_size, group_size, capacity),
        ),
    )
    return blocks.reshape(count_bins, 4, TILE * plane_cells)


def sample_bins(tiles, upper_index, lower_index):
    count_bins = tiles.shape[0]
    capacity = upper_index.shape[1]
    group_size = group_of(count_bins)
    plane_cells = TILE * TILE

    def sample_block(pieces):
        tile_block, upper_block, lower_block = pieces
        lower_hot = (
            lower_block[:, None, :] == lax.broadcasted_iota(jnp.int32, (1, plane_cells, 1), 1)
        ).astype(jnp.float32)
        planes = jnp.einsum(
            "gul,glp->gup",
            tile_block.reshape(group_size, 3 * TILE, plane_cells),
            lower_hot,
            precision=lax.Precision.HIGHEST,
            preferred_element_type=jnp.float32,
        )
        upper_hot = (
            upper_block[:, None, :] == lax.broadcasted_iota(jnp.int32, (1, TILE, 1), 1)
        ).astype(jnp.float32)
        return jnp.sum(
            planes.reshape(group_size, 3, TILE, capacity) * upper_hot[:, None, :, :], axis=2
        )

    blocks = lax.map(
        sample_block,
        (
            tiles.reshape(count_bins // group_size, group_size, 3, TILE * plane_cells),
            upper_index.reshape(count_bins // group_size, group_size, capacity),
            lower_index.reshape(count_bins // group_size, group_size, capacity),
        ),
    )
    return blocks.reshape(count_bins, 3, capacity)


def into_slots(partials, owner_slots):
    hot_slots = (owner_slots[None, :] == lax.broadcasted_iota(jnp.int32, (TPD, 1), 0)).astype(
        jnp.float32
    )
    return jnp.dot(
        hot_slots,
        partials.reshape(partials.shape[0], -1),
        precision=lax.Precision.HIGHEST,
        preferred_element_type=jnp.float32,
    )


def from_slots(tiles_flat, slot_index):
    hot_rows = (slot_index[:, None] == lax.broadcasted_iota(jnp.int32, (1, TPD), 1)).astype(
        jnp.float32
    )
    picked = jnp.dot(
        hot_rows,
        tiles_flat.reshape(TPD, -1),
        precision=lax.Precision.HIGHEST,
        preferred_element_type=jnp.float32,
    )
    return picked.reshape(slot_index.shape[0], 3, -1)


def stack_rows(pieces):
    return tuple(
        (
            jnp.concatenate([portion[member] for portion in pieces], axis=0)
            for member in range(len(pieces[0]))
        )
    )


def take_rows(bundle, begin_row, length):
    return tuple(
        (lax.slice_in_dim(member, begin_row, begin_row + length, axis=0) for member in bundle)
    )


def bucket_rows(values, number):
    return lax.slice_in_dim(
        values, SELF_BINS + number * NBR_BINS, SELF_BINS + (number + 1) * NBR_BINS, axis=0
    )


def move_out(bundle, direction, orient):
    if direction == 0:
        return from_behind(bundle, "gx", orient)
    if direction == 1:
        return from_behind(bundle, "gy", orient)
    return from_behind(bundle, "gz", orient)


def move_back(bundle, direction, orient):
    if direction == 0:
        return from_behind(bundle, "gx", orient)
    if direction == 1:
        return from_behind(bundle, "gy", orient)
    return from_behind(bundle, "gz", orient)


def sectioned_route(buckets):
    holding = {relative: buckets[number] for number, relative in enumerate(neighbour_steps)}
    record = []
    for direction in range(3):
        for orient in (1, -1):
            leaving = [relative for relative in sorted(holding) if relative[direction] == orient]
            arrived = move_out(
                stack_rows([holding[relative] for relative in leaving]), direction, orient
            )
            remaining = {
                relative: holding[relative] for relative in holding if relative[direction] != orient
            }
            entries = []
            begin_row = 0
            for relative in leaving:
                length = holding[relative][0].shape[0]
                portion = take_rows(arrived, begin_row, length)
                begin_row = begin_row + length
                target = tuple(
                    (0 if position == direction else relative[position] for position in range(3))
                )
                if target in remaining:
                    entries.append((relative, length, target, remaining[target][0].shape[0]))
                    remaining[target] = stack_rows([remaining[target], portion])
                else:
                    entries.append((relative, length, target, 0))
                    remaining[target] = portion
            holding = remaining
            record.append((direction, orient, entries))
    own_lengths = [bucket[0].shape[0] for bucket in buckets]

    def answer(replies):
        giving = {(0, 0, 0): replies}
        for direction, orient, entries in reversed(record):
            bundle = stack_rows(
                [
                    take_rows(giving[target], offset, length)
                    for relative, length, target, offset in entries
                ]
            )
            returned = move_back(bundle, direction, -orient)
            begin_row = 0
            for relative, length, target, offset in entries:
                giving[relative] = take_rows(returned, begin_row, length)
                begin_row = begin_row + length
        return [
            take_rows(giving[relative], 0, own_lengths[number])
            for number, relative in enumerate(neighbour_steps)
        ]

    return (holding[0, 0, 0], answer)


def deliver(buckets):
    return sectioned_route(buckets)


def export_faces(values):
    return jnp.stack(
        [
            values[:, 0],
            values[:, -1],
            values[:, :, 0],
            values[:, :, -1],
            values[:, :, :, 0],
            values[:, :, :, -1],
        ],
        axis=1,
    )


def component_faces(velocity):
    return jnp.stack(
        [
            velocity[:, 0, 0],
            velocity[:, 0, -1],
            velocity[:, 1, :, 0],
            velocity[:, 1, :, -1],
            velocity[:, 2, :, :, 0],
            velocity[:, 2, :, :, -1],
        ],
        axis=1,
    )


def beside(values, face_table, neighbour_rows, facing):
    direction = facing // 2
    chosen_rows = neighbour_rows[:, facing]
    ghost_layer = jnp.where(
        (chosen_rows >= 0)[:, None, None], face_table[jnp.maximum(chosen_rows, 0), facing], 0.0
    )
    ghost_layer = jnp.expand_dims(ghost_layer, direction + 1)
    extent = values.shape[1]
    if facing % 2 == 0:
        return jnp.concatenate(
            [lax.slice_in_dim(values, 1, extent, axis=direction + 1), ghost_layer],
            axis=direction + 1,
        )
    return jnp.concatenate(
        [ghost_layer, lax.slice_in_dim(values, 0, extent - 1, axis=direction + 1)],
        axis=direction + 1,
    )


def beside_all(values, face_table, neighbour_rows):
    summed = beside(values, face_table, neighbour_rows, 0)
    for facing in range(1, 6):
        summed = summed + beside(values, face_table, neighbour_rows, facing)
    return summed


def pressure_table(pressure):
    local_faces = export_faces(pressure).reshape(TPD, 6, TILE * TILE)
    gathered = with_halo(local_faces[None, None, None], (("gx", 0), ("gy", 1), ("gz", 2)), 1)
    return gathered.reshape(27 * TPD, 6, TILE, TILE)


def velocity_table_of(local_faces, coord_values):
    face_block, coord_block = (
        with_halo(local_faces[None, None, None], (("gx", 0), ("gy", 1), ("gz", 2)), 1),
        with_halo(coord_values[None, None, None], (("gx", 0), ("gy", 1), ("gz", 2)), 1),
    )
    return (
        face_block.reshape(27 * TPD, 6, TILE, TILE),
        jnp.transpose(coord_block, (0, 1, 2, 4, 3)).reshape(27 * TPD, 3),
    )


def find_rows(coord_values, candidates):
    listing = []
    for relative in face_steps:
        wanted = coord_values + jnp.array(relative, dtype=jnp.float32)[:, None]
        matches = jnp.all(candidates[None, :, :] == jnp.transpose(wanted)[:, None, :], axis=2)
        located = jnp.any(matches, axis=1)
        position = jnp.sum(
            jnp.where(matches, lax.broadcasted_iota(jnp.int32, matches.shape, 1), 0), axis=1
        )
        listing.append(jnp.where(located, position, -1))
    return jnp.stack(listing, axis=1)


def local(
    tile_coords,
    owner_map,
    bin_tile,
    bin_count,
    part_cell,
    part_offset,
    part_velocity,
    part_affine,
    part_mass,
):
    plane_cells = TILE * TILE
    total_cells = TILE * plane_cells
    own_bins = SELF_BINS
    owner_slots = owner_map[bin_tile] % TPD
    living = lax.broadcasted_iota(jnp.int32, part_cell.shape, 1) < bin_count[:, None]
    amounts = deposits(part_offset, part_velocity, part_affine, part_mass, living)
    upper_index = part_cell // plane_cells
    lower_index = part_cell % plane_cells
    slot_values = owner_slots.astype(jnp.float32)
    partials = splat_bins(amounts, upper_index, lower_index)
    totals = into_slots(partials[:own_bins], owner_slots[:own_bins])
    buckets = [
        (bucket_rows(partials, number), bucket_rows(slot_values, number)) for number in range(26)
    ]
    arrived, answer = deliver(buckets)
    got_partials, got_slots = arrived
    got_slot_index = got_slots.astype(jnp.int32)
    totals = totals + into_slots(got_partials, got_slot_index)
    totals = totals.reshape(TPD, 4, TILE, TILE, TILE)
    masses = totals[:, 0]
    fluid_mask = masses > 0.0
    safe_mass = jnp.where(fluid_mask, masses, 1.0)
    velocity = jnp.where(fluid_mask[:, None], totals[:, 1:] / safe_mass[:, None], 0.0)
    upward = jnp.array([0.0, 1.0, 0.0], dtype=jnp.float32)
    velocity = (
        velocity
        - gravity_step * fluid_mask.astype(jnp.float32)[:, None] * upward[None, :, None, None, None]
    )
    coord_values = (tile_coords + 1).astype(jnp.float32)
    local_faces = component_faces(velocity).reshape(TPD, 6, plane_cells)
    velocity_table, candidates = velocity_table_of(local_faces, coord_values)
    neighbour_rows = find_rows(coord_values, candidates)
    diverge = 0.5 * (
        beside(velocity[:, 0], velocity_table, neighbour_rows, 0)
        - beside(velocity[:, 0], velocity_table, neighbour_rows, 1)
    )
    diverge = diverge + 0.5 * (
        beside(velocity[:, 1], velocity_table, neighbour_rows, 2)
        - beside(velocity[:, 1], velocity_table, neighbour_rows, 3)
    )
    diverge = diverge + 0.5 * (
        beside(velocity[:, 2], velocity_table, neighbour_rows, 4)
        - beside(velocity[:, 2], velocity_table, neighbour_rows, 5)
    )
    pressure = jnp.where(fluid_mask, (0.0 - diverge) / 6.0, 0.0)
    for sweep_number in range(SWEEPS - 1):
        face_table = pressure_table(pressure)
        pressure = jnp.where(
            fluid_mask, (beside_all(pressure, face_table, neighbour_rows) - diverge) / 6.0, 0.0
        )
    face_table = pressure_table(pressure)
    gradient = jnp.stack(
        [
            0.5
            * (
                beside(pressure, face_table, neighbour_rows, 2 * component)
                - beside(pressure, face_table, neighbour_rows, 2 * component + 1)
            )
            for component in range(3)
        ],
        axis=1,
    )
    velocity = jnp.where(fluid_mask[:, None], velocity - gradient, 0.0)
    tiles_flat = velocity.reshape(TPD, 3, total_cells)
    flat_velocity = jnp.transpose(tiles_flat, (1, 0, 2)).reshape(3, TPD * total_cells)
    near_values = sample_bins(
        from_slots(tiles_flat, owner_slots[:own_bins]),
        upper_index[:own_bins],
        lower_index[:own_bins],
    )
    replies = (from_slots(tiles_flat, got_slot_index),)
    remote_tiles = stack_rows(answer(replies))[0]
    remote = sample_bins(remote_tiles, upper_index[own_bins:], lower_index[own_bins:])
    sampled = jnp.concatenate([near_values, remote], axis=0)
    particle_velocity = jnp.where(living[:, None, :], sampled, 0.0)
    return (flat_velocity, pressure.reshape(-1), particle_velocity)


def solution(mesh):
    placed = (
        P(None, ("gx", "gy", "gz")),
        P(),
        P(("gx", "gy", "gz")),
        P(("gx", "gy", "gz")),
        P(("gx", "gy", "gz"), None),
        P(("gx", "gy", "gz"), None, None),
        P(("gx", "gy", "gz"), None, None),
        P(("gx", "gy", "gz"), None, None),
        P(("gx", "gy", "gz"), None),
    )
    return jax.shard_map(
        local,
        mesh=mesh,
        in_specs=placed,
        out_specs=(
            P(None, ("gx", "gy", "gz")),
            P(("gx", "gy", "gz")),
            P(("gx", "gy", "gz"), None, None),
        ),
        check_vma=False,
    )
```

profile of v0, /device:TPU:0, one launch (start us, length us, event | category | flops | bytes accessed | tf_op | source)
XLA Modules:
  0.0 585.1 jit_solution(1827026243003489105)
XLA Ops:
  1.3 5.0 collective-permute-start.12
  21.9 73.7 %while.30 = (s32[]{:T(128)}, f32[29,2,4,512]{3,2,1,0:T(4,128)}, bf16[29,2,4,2048]{3,2,1,0:T(4,128)(2,1)}, s32[29,2,2048]{2,1,0:T(2,128)}, s32[29,2,2048]{2,1,0:T(2,128)}, /*index=5*/s32[]{:T(128)}) while((s32[]{:T(128)}, f32[29,2,4,512]{3,2,1,0:T(4,128)}, bf16[29,2,4,2048]{3,2,1,0:T(4,128)(2,1)}, s32[29,2,2048]{2,1,0:T(2,128)}, ...), condition=%wide.region_1.2_spmd, body=%wide.region_0.1_spmd.sunk | while | flops 17235968 | bytes 410189 | solution.py:87
  110.7 5.6 collective-permute-start
  118.2 5.7 concatenate.326
  125.2 5.6 concatenate.325
  180.6 4.8 collective-permute-start.18
  187.1 5.4 collective-permute-done.19
  210.1 7.4 %reshape.1166 = f32[432,6,8,8]{3,2,1,0:T(8,128)} reshape(f32[3,3,3,16,6,64]{5,4,3,2,1,0:T(8,128)} %copy.412) | data formatting | bytes 1327104 | tf_op jit(solution)/shard_map/reshape | solution.py:319
  217.5 4.6 gather_fusion.1
  222.3 4.6 gather_fusion.2
  227.1 4.6 gather_fusion.3
  250.8 4.8 collective-permute-start.24
  277.5 7.4 %reshape.1167 = f32[432,6,8,8]{3,2,1,0:T(8,128)} reshape(f32[3,3,3,16,6,64]{5,4,3,2,1,0:T(8,128)} %copy.414) | data formatting | bytes 1327104 | tf_op jit(solution)/shard_map/reshape | solution.py:310
  284.9 5.2 gather_fusion.12
  294.7 4.6 gather_fusion.10
  299.3 4.6 gather_fusion.9
  303.9 4.6 gather_fusion.8
  308.5 4.6 gather_fusion.7
  348.0 7.4 %reshape.1168 = f32[432,6,8,8]{3,2,1,0:T(8,128)} reshape(f32[3,3,3,16,6,64]{5,4,3,2,1,0:T(8,128)} %copy.416) | data formatting | bytes 1327104 | tf_op jit(solution)/shard_map/reshape | solution.py:310
  355.3 5.2 gather_fusion.18
  365.1 4.6 gather_fusion.16
  369.7 4.6 gather_fusion.15
  418.2 7.4 %reshape.1169 = f32[432,6,8,8]{3,2,1,0:T(8,128)} reshape(f32[3,3,3,16,6,64]{5,4,3,2,1,0:T(8,128)} %copy.418) | data formatting | bytes 1327104 | tf_op jit(solution)/shard_map/reshape | solution.py:310
  425.6 4.6 gather_fusion.19
  434.8 4.6 gather_fusion.21
  439.4 4.6 gather_fusion.22
  444.0 4.6 gather_fusion.23
  448.6 4.6 gather_fusion.24
  487.0 7.4 %reshape.1170 = f32[432,6,8,8]{3,2,1,0:T(8,128)} reshape(f32[3,3,3,16,6,64]{5,4,3,2,1,0:T(8,128)} %copy.420) | data formatting | bytes 1327104 | tf_op jit(solution)/shard_map/reshape | solution.py:310
  494.4 4.6 gather_fusion.26
  550.7 11.5 %while.31 = (s32[]{:T(128)}, f32[4,8,3,2048]{3,1,0,2:T(8,128)}, f32[4,8,3,512]{3,1,2,0:T(8,128)S(1)}, s32[4,8,2048]{2,1,0:T(8,128)S(1)}, s32[4,8,2048]{2,1,0:T(8,128)S(1)}, /*index=5*/s32[]{:T(128)}) while((s32[]{:T(128)}, f32[4,8,3,2048]{3,1,0,2:T(8,128)}, f32[4,8,3,512]{3,1,2,0:T(8,128)S(1)}, s32[4,8,2048]{2,1,0:T(8,128)S(1)}, ...), condition=%wide.region_22.23_spmd, body=%wide.region_20.22_spmd.sunk | while | flops 304037888 | bytes 2376269 | solution.py:123
  563.1 18.6 %while.32 = (s32[]{:T(128)}, f32[13,2,3,2048]{3,2,1,0:T(4,128)S(1)}, f32[13,2,3,512]{3,2,1,0:T(4,128)S(1)}, s32[13,2,2048]{2,1,0:T(2,128)}, s32[13,2,2048]{2,1,0:T(2,128)}, /*index=5*/s32[]{:T(128)}) while((s32[]{:T(128)}, f32[13,2,3,2048]{3,2,1,0:T(4,128)S(1)}, f32[13,2,3,512]{3,2,1,0:T(4,128)S(1)}, s32[13,2,2048]{2,1,0:T(2,128)}, ...), condition=%wide.region_25.26_spmd, body=%wide.region_23.25_spmd.sunk | while | flops 76009472 | bytes 602193 | solution.py:123
  (808 shorter events, 428.1 us)
Async XLA Ops:
  1.3 129.5 %collective-permute-start.12 = (f32[1,1,1,3,16]{4,3,2,1,0:T(4,128)S(1)}, f32[1,1,1,3,16]{4,3,2,1,0:T(4,128)S(1)}, u32[]{:S(2)}, u32[]{:S(2)}) collective-permute-start(f32[1,1,1,3,16]{4,3,2,1,0:T(4,128)S(1)} %convert_bitcast_fusion), channel_id=1, source_target_pairs={{0,8},{8,16},{16,24},{1,9},{9,17},{17,25},{2,10},{10,18},{18,26},{... | collective-permute-start | bytes 584 | tf_op jit(solution)/shard_map/ppermute | solution.py:35
  6.3 129.0 %collective-permute-start.13 = (f32[1,1,1,3,16]{4,3,2,1,0:T(4,128)S(1)}, f32[1,1,1,3,16]{4,3,2,1,0:T(4,128)S(1)}, u32[]{:S(2)}, u32[]{:S(2)}) collective-permute-start(f32[1,1,1,3,16]{4,3,2,1,0:T(4,128)S(1)} %convert_bitcast_fusion), channel_id=1, source_target_pairs={{8,0},{16,8},{24,16},{9,1},{17,9},{25,17},{10,2},{18,10},{26,18},{... | collective-permute-start | bytes 584 | tf_op jit(solution)/shard_map/ppermute | solution.py:38
  96.5 66.1 %collective-permute-start.6 = (f32[9,4,512]{2,1,0:T(4,128)S(1)}, f32[9,4,512]{2,1,0:T(4,128)S(1)}, u32[]{:S(2)}, u32[]{:S(2)}) collective-permute-start(f32[9,4,512]{2,1,0:T(4,128)S(1)} %get-tuple-element.186), channel_id=1, source_target_pairs={{0,8},{8,16},{16,24},{1,9},{9,17},{17,25},{2,10},{10,18},{18,26},{... | collective-permute-start | bytes 221192 | tf_op jit(solution)/shard_map/ppermute | solution.py:27
  101.1 61.6 %collective-permute-start.7 = (f32[9,4,512]{2,1,0:T(4,128)S(1)}, f32[9,4,512]{2,1,0:T(4,128)S(1)}, u32[]{:S(2)}, u32[]{:S(2)}) collective-permute-start(f32[9,4,512]{2,1,0:T(4,128)S(1)} %get-tuple-element.185), channel_id=1, source_target_pairs={{8,0},{16,8},{24,16},{9,1},{17,9},{25,17},{10,2},{18,10},{26,18},{... | collective-permute-start | bytes 221192 | tf_op jit(solution)/shard_map/ppermute | solution.py:27
  103.3 7.4 %collective-permute-start.1 = (f32[9]{0:T(128)S(1)}, f32[9]{0:T(128)S(1)}, u32[]{:S(2)}, u32[]{:S(2)}) collective-permute-start(f32[9]{0:T(128)S(1)} %get-tuple-element.327), channel_id=1, source_target_pairs={{8,0},{16,8},{24,16},{9,1},{17,9},{25,17},{10,2},{18,10},{26,18},{... | collective-permute-start | bytes 116 | tf_op jit(solution)/shard_map/ppermute | solution.py:27
  110.7 6.8 %collective-permute-start = (f32[9]{0:T(128)S(1)}, f32[9]{0:T(128)S(1)}, u32[]{:S(2)}, u32[]{:S(2)}) collective-permute-start(f32[9]{0:T(128)S(1)} %get-tuple-element.328), channel_id=1, source_target_pairs={{0,8},{8,16},{16,24},{1,9},{9,17},{17,25},{2,10},{10,18},{18,26},{... | collective-permute-start | bytes 116 | tf_op jit(solution)/shard_map/ppermute | solution.py:27
  123.9 15.0 %collective-permute-start.3 = (f32[9]{0:T(128)S(1)}, f32[9]{0:T(128)S(1)}, u32[]{:S(2)}, u32[]{:S(2)}) collective-permute-start(f32[9]{0:T(128)S(1)} %concatenate.326), channel_id=1, source_target_pairs={{2,0},{4,2},{6,4},{3,1},{5,3},{7,5},{10,8},{12,10},{14,12},{11,9},... | collective-permute-start | bytes 116 | tf_op jit(solution)/shard_map/ppermute | solution.py:27
  130.8 16.2 %collective-permute-start.2 = (f32[9]{0:T(128)S(1)}, f32[9]{0:T(128)S(1)}, u32[]{:S(2)}, u32[]{:S(2)}) collective-permute-start(f32[9]{0:T(128)S(1)} %concatenate.325), channel_id=1, source_target_pairs={{0,2},{2,4},{4,6},{1,3},{3,5},{5,7},{8,10},{10,12},{12,14},{9,11},... | collective-permute-start | bytes 116 | tf_op jit(solution)/shard_map/ppermute | solution.py:27
  135.4 4.9 collective-permute-start.14
  138.9 5.5 collective-permute-start.15
  144.4 14.0 %collective-permute-start.16 = (f32[3,3,1,3,16]{4,3,2,1,0:T(4,128)S(1)}, f32[3,3,1,3,16]{4,3,2,1,0:T(4,128)S(1)}, u32[]{:S(2)}, u32[]{:S(2)}) collective-permute-start(f32[3,3,1,3,16]{4,3,2,1,0:T(4,128)S(1)} %pad_maximum_fusion.17), channel_id=1, source_target_pairs={{0,1},{2,3},{4,5},{6,7},{8,9},{10,11},{12,13},{14,15},{16,17},{18,... | collective-permute-start | bytes 5192 | tf_op jit(solution)/shard_map/ppermute | solution.py:35
  145.7 12.7 %collective-permute-start.17 = (f32[3,3,1,3,16]{4,3,2,1,0:T(4,128)S(1)}, f32[3,3,1,3,16]{4,3,2,1,0:T(4,128)S(1)}, u32[]{:S(2)}, u32[]{:S(2)}) collective-permute-start(f32[3,3,1,3,16]{4,3,2,1,0:T(4,128)S(1)} %pad_maximum_fusion.17), channel_id=1, source_target_pairs={{1,0},{3,2},{5,4},{7,6},{9,8},{11,10},{13,12},{15,14},{17,16},{19,... | collective-permute-start | bytes 5192 | tf_op jit(solution)/shard_map/ppermute | solution.py:38
  149.1 5.1 collective-permute-start.4
  164.2 5.5 collective-permute-start.8
  167.7 6.2 %collective-permute-start.9 = (f32[9,4,512]{2,1,0:T(4,128)S(1)}, f32[9,4,512]{2,1,0:T(4,128)S(1)}, u32[]{:S(2)}, u32[]{:S(2)}) collective-permute-start(f32[9,4,512]{2,1,0:T(4,128)S(1)} %get-tuple-element.273), channel_id=1, source_target_pairs={{2,0},{4,2},{6,4},{3,1},{5,3},{7,5},{10,8},{12,10},{14,12},{11,9},... | collective-permute-start | bytes 221192 | tf_op jit(solution)/shard_map/ppermute | solution.py:27
  180.6 6.6 %collective-permute-start.18 = (f32[1,1,1,16,6,64]{5,3,4,2,1,0:T(8,128)S(1)}, f32[1,1,1,16,6,64]{5,3,4,2,1,0:T(8,128)S(1)}, u32[]{:S(2)}, u32[]{:S(2)}) collective-permute-start(f32[1,1,1,16,6,64]{5,3,4,2,1,0:T(8,128)S(1)} %constant_dynamic-update-slice_fusion.35), channel_id=1, source_target_pairs={{0,8},{8,16},{16,24},{1,9},{9,17},{17,25},{2,10},{10,18},{18,26},{... | collective-permute-start | bytes 73736 | tf_op jit(solution)/shard_map/ppermute | solution.py:35
  185.4 7.1 %collective-permute-start.19 = (f32[1,1,1,16,6,64]{5,3,4,2,1,0:T(8,128)S(1)}, f32[1,1,1,16,6,64]{5,3,4,2,1,0:T(8,128)S(1)}, u32[]{:S(2)}, u32[]{:S(2)}) collective-permute-start(f32[1,1,1,16,6,64]{5,3,4,2,1,0:T(8,128)S(1)} %constant_dynamic-update-slice_fusion.35), channel_id=1, source_target_pairs={{8,0},{16,8},{24,16},{9,1},{17,9},{25,17},{10,2},{18,10},{26,18},{... | collective-permute-start | bytes 73736 | tf_op jit(solution)/shard_map/ppermute | solution.py:38
  193.2 4.9 collective-permute-start.20
  195.1 7.2 %collective-permute-start.21 = (f32[3,1,1,16,6,64]{5,3,4,2,1,0:T(8,128)}, f32[3,1,1,16,6,64]{5,3,4,2,1,0:T(8,128)S(1)}, u32[]{:S(2)}, u32[]{:S(2)}) collective-permute-start(f32[3,1,1,16,6,64]{5,3,4,2,1,0:T(8,128)} %pad_maximum_fusion.10), channel_id=1, source_target_pairs={{2,0},{4,2},{6,4},{3,1},{5,3},{7,5},{10,8},{12,10},{14,12},{11,9},... | collective-permute-start | bytes 221192 | tf_op jit(solution)/shard_map/ppermute | solution.py:38
  250.8 6.6 %collective-permute-start.24 = (f32[1,1,1,16,6,64]{5,3,4,2,1,0:T(8,128)S(1)}, f32[1,1,1,16,6,64]{5,3,4,2,1,0:T(8,128)S(1)}, u32[]{:S(2)}, u32[]{:S(2)}) collective-permute-start(f32[1,1,1,16,6,64]{5,3,4,2,1,0:T(8,128)S(1)} %constant_dynamic-update-slice_fusion.41), channel_id=1, source_target_pairs={{0,8},{8,16},{16,24},{1,9},{9,17},{17,25},{2,10},{10,18},{18,26},{... | collective-permute-start | bytes 73736 | tf_op jit(solution)/shard_map/ppermute | solution.py:35
  255.6 6.0 %collective-permute-start.25 = (f32[1,1,1,16,6,64]{5,3,4,2,1,0:T(8,128)S(1)}, f32[1,1,1,16,6,64]{5,3,4,2,1,0:T(8,128)S(1)}, u32[]{:S(2)}, u32[]{:S(2)}) collective-permute-start(f32[1,1,1,16,6,64]{5,3,4,2,1,0:T(8,128)S(1)} %constant_dynamic-update-slice_fusion.41), channel_id=1, source_target_pairs={{8,0},{16,8},{24,16},{9,1},{17,9},{25,17},{10,2},{18,10},{26,18},{... | collective-permute-start | bytes 73736 | tf_op jit(solution)/shard_map/ppermute | solution.py:38
  263.6 7.0 %collective-permute-start.27 = (f32[3,1,1,16,6,64]{5,3,4,2,1,0:T(8,128)S(1)}, f32[3,1,1,16,6,64]{5,3,4,2,1,0:T(8,128)S(1)}, u32[]{:S(2)}, u32[]{:S(2)}) collective-permute-start(f32[3,1,1,16,6,64]{5,3,4,2,1,0:T(8,128)S(1)} %pad_maximum_fusion.11), channel_id=1, source_target_pairs={{2,0},{4,2},{6,4},{3,1},{5,3},{7,5},{10,8},{12,10},{14,12},{11,9},... | collective-permute-start | bytes 221192 | tf_op jit(solution)/shard_map/ppermute | solution.py:38
  326.1 6.0 %collective-permute-start.31 = (f32[1,1,1,16,6,64]{5,3,4,2,1,0:T(8,128)S(1)}, f32[1,1,1,16,6,64]{5,3,4,2,1,0:T(8,128)S(1)}, u32[]{:S(2)}, u32[]{:S(2)}) collective-permute-start(f32[1,1,1,16,6,64]{5,3,4,2,1,0:T(8,128)S(1)} %constant_dynamic-update-slice_fusion.47), channel_id=1, source_target_pairs={{8,0},{16,8},{24,16},{9,1},{17,9},{25,17},{10,2},{18,10},{26,18},{... | collective-permute-start | bytes 73736 | tf_op jit(solution)/shard_map/ppermute | solution.py:38
  334.0 7.0 %collective-permute-start.33 = (f32[3,1,1,16,6,64]{5,3,4,2,1,0:T(8,128)S(1)}, f32[3,1,1,16,6,64]{5,3,4,2,1,0:T(8,128)S(1)}, u32[]{:S(2)}, u32[]{:S(2)}) collective-permute-start(f32[3,1,1,16,6,64]{5,3,4,2,1,0:T(8,128)S(1)} %pad_maximum_fusion.12), channel_id=1, source_target_pairs={{2,0},{4,2},{6,4},{3,1},{5,3},{7,5},{10,8},{12,10},{14,12},{11,9},... | collective-permute-start | bytes 221192 | tf_op jit(solution)/shard_map/ppermute | solution.py:38
  396.3 6.0 %collective-permute-start.37 = (f32[1,1,1,16,6,64]{5,3,4,2,1,0:T(8,128)S(1)}, f32[1,1,1,16,6,64]{5,3,4,2,1,0:T(8,128)S(1)}, u32[]{:S(2)}, u32[]{:S(2)}) collective-permute-start(f32[1,1,1,16,6,64]{5,3,4,2,1,0:T(8,128)S(1)} %constant_dynamic-update-slice_fusion.53), channel_id=1, source_target_pairs={{8,0},{16,8},{24,16},{9,1},{17,9},{25,17},{10,2},{18,10},{26,18},{... | collective-permute-start | bytes 73736 | tf_op jit(solution)/shard_map/ppermute | solution.py:38
  404.3 7.0 %collective-permute-start.39 = (f32[3,1,1,16,6,64]{5,3,4,2,1,0:T(8,128)S(1)}, f32[3,1,1,16,6,64]{5,3,4,2,1,0:T(8,128)S(1)}, u32[]{:S(2)}, u32[]{:S(2)}) collective-permute-start(f32[3,1,1,16,6,64]{5,3,4,2,1,0:T(8,128)S(1)} %pad_maximum_fusion.13), channel_id=1, source_target_pairs={{2,0},{4,2},{6,4},{3,1},{5,3},{7,5},{10,8},{12,10},{14,12},{11,9},... | collective-permute-start | bytes 221192 | tf_op jit(solution)/shard_map/ppermute | solution.py:38
  459.5 5.7 collective-permute-start.42
  462.3 6.0 %collective-permute-start.43 = (f32[1,1,1,16,6,64]{5,3,4,2,1,0:T(8,128)S(1)}, f32[1,1,1,16,6,64]{5,3,4,2,1,0:T(8,128)S(1)}, u32[]{:S(2)}, u32[]{:S(2)}) collective-permute-start(f32[1,1,1,16,6,64]{5,3,4,2,1,0:T(8,128)S(1)} %constant_dynamic-update-slice_fusion.59), channel_id=1, source_target_pairs={{8,0},{16,8},{24,16},{9,1},{17,9},{25,17},{10,2},{18,10},{26,18},{... | collective-permute-start | bytes 73736 | tf_op jit(solution)/shard_map/ppermute | solution.py:38
  469.0 4.9 collective-permute-start.44
  470.9 7.4 %collective-permute-start.45 = (f32[3,1,1,16,6,64]{5,3,4,2,1,0:T(8,128)}, f32[3,1,1,16,6,64]{5,3,4,2,1,0:T(8,128)}, u32[]{:S(2)}, u32[]{:S(2)}) collective-permute-start(f32[3,1,1,16,6,64]{5,3,4,2,1,0:T(8,128)} %pad_maximum_fusion.14), channel_id=1, source_target_pairs={{2,0},{4,2},{6,4},{3,1},{5,3},{7,5},{10,8},{12,10},{14,12},{11,9},... | collective-permute-start | bytes 221192 | tf_op jit(solution)/shard_map/ppermute | solution.py:38
  537.9 6.2 %collective-permute-start.51 = (f32[9,3,512]{2,1,0:T(4,128)S(1)}, f32[9,3,512]{2,1,0:T(4,128)S(1)}, u32[]{:S(2)}, u32[]{:S(2)}) collective-permute-start(f32[9,3,512]{2,1,0:T(4,128)S(1)} %pad_maximum_fusion.16), channel_id=1, source_target_pairs={{2,0},{4,2},{6,4},{3,1},{5,3},{7,5},{10,8},{12,10},{14,12},{11,9},... | collective-permute-start | bytes 165896 | tf_op jit(solution)/shard_map/ppermute | solution.py:27
  549.1 14.0 %collective-permute-start.53 = (f32[9,3,512]{2,1,0:T(4,128)S(1)}, f32[9,3,512]{2,1,0:T(4,128)S(1)}, u32[]{:S(2)}, u32[]{:S(2)}) collective-permute-start(f32[9,3,512]{2,1,0:T(4,128)S(1)} %get-tuple-element.245), channel_id=1, source_target_pairs={{8,0},{16,8},{24,16},{9,1},{17,9},{25,17},{10,2},{18,10},{26,18},{... | collective-permute-start | bytes 165896 | tf_op jit(solution)/shard_map/ppermute | solution.py:27
  (72 other events, 1193.6 us)
where the time goes:
time: 596 us; the launch traced here: 585 us
  local copies, waits for them, and re-layouts  330 us (55%)
  starting transfers between devices  109 us (18%)
  waiting for transfers between devices  75.3 us (13%)
  other arithmetic  42.8 us (7%)
  matrix products  24.6 us (4%)
    gather x30, local copies, waits for them, and re-layouts, beside(): face_table[jnp.maximum(chosen_rows, 0), facing]  139 us
    ppermute x18, waiting for transfers between devices, with_halo(): lax.ppermute(lax.slice_in_dim(block, 0, width, axis=dim), axis, backward)  54.9 us
    ppermute x18, starting transfers between devices, with_halo(): lax.ppermute(lax.slice_in_dim(block, block.shape[dim] - width, None, axis...  44.2 us
    ppermute x18, starting transfers between devices, from_behind(): return lax.ppermute(block, axis, route)  41.1 us
    reshape x8, local copies, waits for them, and re-layouts, pressure_table(): return gathered.reshape(27 * TPD, 6, TILE, TILE)  36.4 us
    ppermute x18, starting transfers between devices, with_halo(): lax.ppermute(lax.slice_in_dim(block, 0, width, axis=dim), axis, backward)  23.7 us
    mul x29, local copies, waits for them, and re-layouts, splat_block(): amount_block[:, :, None, :] * upper_hot[:, None, :, :]  22.5 us
    eq x29, local copies, waits for them, and re-layouts, splat_block(): lower_block[:, :, None]  21.4 us
  transfers between devices with their start and end apart: 54, of which 33 were waited for; matrix products, arithmetic and copies ran while one was open for 24% of the time, Pallas kernels for 0%

commit v1 on v0

v1 whole, which is shorter than its diff:
```python
import functools

import jax
import jax.numpy as jnp
from jax import lax
from jax.experimental import pallas as pl
from jax.experimental.pallas import tpu as pltpu
from jax.sharding import PartitionSpec as P

TILE = 8
SELF_BINS = 32
SWEEPS = 4
CELLS = TILE * TILE * TILE
LANES = 128
GROUPS = CELLS // LANES
QROWS = 4 * GROUPS
BLOCK = QROWS + 8
STEP_BINS = 8
GRAVITY = 0.5
AXES = ("gx", "gy", "gz")
MESH = pl.DeviceIdType.MESH

OFFSETS = [
    (x, y, z)
    for x in (-1, 0, 1)
    for y in (-1, 0, 1)
    for z in (-1, 0, 1)
    if (x, y, z) != (0, 0, 0)
]
FACES = [(1, 0, 0), (-1, 0, 0), (0, 1, 0), (0, -1, 0), (0, 0, 1), (0, 0, -1)]


def lower_hot(cell_row):
    points = cell_row.shape[1]
    low = (cell_row & (LANES - 1)).astype(jnp.float32).astype(jnp.bfloat16)
    rows = lax.broadcasted_iota(jnp.int32, (LANES, points), 0)
    rows = rows.astype(jnp.float32).astype(jnp.bfloat16)
    return jnp.where(rows == low, jnp.bfloat16(1), jnp.bfloat16(0))


def upper_row(cell_row, count):
    lane = lax.broadcasted_iota(jnp.int32, cell_row.shape, 1)
    return jnp.where(lane < count, cell_row >> 7, -1)


def bins_of_step(step, bins, body):
    left = jnp.minimum(STEP_BINS, bins - step * STEP_BINS)
    unroll = 2 if bins % 2 == 0 else 1

    def pair(i, carry):
        for k in range(unroll):
            body(i * unroll + k)
        return carry

    lax.fori_loop(0, left // unroll, pair, 0)


def splat_kernel(
    bins, slots_of, owner, tile, count, cell, offset, velocity, affine, mass, out
):
    step = pl.program_id(0)

    def one(j):
        b = step * STEP_BINS + j
        points = cell.shape[1]
        cells = cell[pl.ds(j, 1), :]
        m = mass[pl.ds(j, 1), :]
        moved = []
        for a in range(3):
            drift = affine[j, pl.ds(3 * a, 1), :] * offset[j, pl.ds(0, 1), :]
            for e in (1, 2):
                drift = drift + affine[j, pl.ds(3 * a + e, 1), :] * offset[j, pl.ds(e, 1), :]
            moved.append(m * (velocity[j, pl.ds(a, 1), :] - drift))
        upper = upper_row(cells, count[b])
        sub = lax.broadcasted_iota(jnp.int32, (8, points), 0)
        hit = (sub & 3) == upper
        first = sub < 4
        halves = []
        for low, high in ((m, moved[0]), (moved[1], moved[2])):
            both = jnp.where(first, low, high)
            halves.append(jnp.where(hit, both, 0.0))
        weighted = jnp.concatenate(halves, axis=0).astype(jnp.bfloat16)
        summed = lax.dot_general(
            weighted,
            lower_hot(cells),
            (((1,), (1,)), ((), ())),
            preferred_element_type=jnp.float32,
        )
        base = pl.multiple_of(j * BLOCK, 8)
        out[pl.ds(base, QROWS), :] = summed
        slot = lax.rem(owner[tile[b]], slots_of).astype(jnp.float32)
        out[pl.ds(base + QROWS, 8), :] = jnp.full((8, LANES), slot, jnp.float32)

    bins_of_step(step, bins, one)


def sample_kernel(bins, slots_of, owner, tile, count, cell, table, out):
    step = pl.program_id(0)

    def one(j):
        b = step * STEP_BINS + j
        points = cell.shape[1]
        cells = cell[pl.ds(j, 1), :]
        slot = lax.rem(owner[tile[b]], slots_of)
        place = jnp.where(b < SELF_BINS, slot, slots_of + b - SELF_BINS)
        rows = table[pl.ds(pl.multiple_of(place * QROWS, 8), QROWS), :].astype(jnp.bfloat16)
        planes = lax.dot_general(
            rows, lower_hot(cells), (((1,), (0,)), ((), ())), preferred_element_type=jnp.float32
        )
        upper = upper_row(cells, count[b])
        half = lax.broadcasted_iota(jnp.int32, (8, points), 0) >> 2
        val = jnp.where(upper == half, planes[0:8], 0.0)
        for k in range(1, GROUPS // 2):
            val = val + jnp.where(upper == half + 2 * k, planes[8 * k : 8 * k + 8], 0.0)
        out[j] = val[0:3] + val[4:7]

    bins_of_step(step, bins, one)


def split(x):
    high = x.astype(jnp.bfloat16)
    low = (x - high.astype(jnp.float32)).astype(jnp.bfloat16)
    return high, low


def pick(hot, x):
    high, low = split(x)
    return jnp.dot(hot, high, preferred_element_type=jnp.float32) + jnp.dot(
        hot, low, preferred_element_type=jnp.float32
    )


def shifted(field, ghost, facing):
    lane = lax.broadcasted_iota(jnp.int32, field.shape, 1)
    stride = (TILE * TILE, TILE, 1)[facing // 2]
    pos = (lane // stride) % TILE
    wrap = stride * (TILE - 1)
    if facing % 2 == 0:
        inner = pltpu.roll(field, CELLS - stride, 1)
        outer = pltpu.roll(ghost, wrap, 1)
        return jnp.where(pos == TILE - 1, outer, inner)
    inner = pltpu.roll(field, stride, 1)
    outer = pltpu.roll(ghost, CELLS - wrap, 1)
    return jnp.where(pos == 0, outer, inner)


def grid_kernel(
    sizes,
    tpd,
    per,
    near_pad,
    lin_row,
    lin_col,
    parts,
    out_vel,
    out_p,
    out_table,
    lins,
    got,
    vel_t,
    p_t,
    reply,
    back,
    part_send,
    part_recv,
    lin_send,
    lin_recv,
    face_send,
    face_recv,
    reply_send,
    reply_recv,
):
    me = [lax.axis_index(name) for name in AXES]

    def inside(rel):
        ok = None
        for n in range(3):
            if rel[n] == 0:
                continue
            one = me[n] < sizes[n] - 1 if rel[n] > 0 else me[n] > 0
            ok = one if ok is None else jnp.logical_and(ok, one)
        return ok

    def at(rel):
        return tuple(
            jnp.clip(me[n] + rel[n], 0, sizes[n] - 1) if rel[n] else me[n] for n in range(3)
        )

    def neg(rel):
        return tuple(-v for v in rel)

    lins[...] = jnp.full(lins.shape, -1, jnp.int32)
    got[...] = jnp.zeros(got.shape, jnp.float32)
    vel_t[...] = jnp.zeros(vel_t.shape, jnp.float32)
    p_t[...] = jnp.zeros(p_t.shape, jnp.float32)
    back[...] = jnp.zeros(back.shape, jnp.float32)

    barrier = pltpu.get_barrier_semaphore()
    for rel in OFFSETS:

        @pl.when(inside(rel))
        def _(rel=rel):
            pl.semaphore_signal(barrier, inc=1, device_id=at(rel), device_id_type=MESH)

    spans = [
        1 + (me[n] > 0).astype(jnp.int32) + (me[n] < sizes[n] - 1).astype(jnp.int32)
        for n in range(3)
    ]
    pl.semaphore_wait(barrier, spans[0] * spans[1] * spans[2] - 1)

    def part_copy(number):
        rows = per * BLOCK
        return pltpu.make_async_remote_copy(
            src_ref=parts.at[pl.ds(SELF_BINS * BLOCK + number * rows, rows)],
            dst_ref=got.at[pl.ds(number * rows, rows)],
            send_sem=part_send.at[number],
            recv_sem=part_recv.at[number],
            device_id=at(OFFSETS[number]),
            device_id_type=MESH,
        )

    def reply_copy(number):
        rows = per * QROWS
        return pltpu.make_async_remote_copy(
            src_ref=reply.at[pl.ds(number * rows, rows)],
            dst_ref=back.at[pl.ds(number * rows, rows)],
            send_sem=reply_send.at[number],
            recv_sem=reply_recv.at[number],
            device_id=at(neg(OFFSETS[number])),
            device_id_type=MESH,
        )

    def lin_copy(d, slot):
        return pltpu.make_async_remote_copy(
            src_ref=lin_row,
            dst_ref=lins.at[slot],
            send_sem=lin_send.at[d],
            recv_sem=lin_recv.at[slot],
            device_id=at(FACES[d]),
            device_id_type=MESH,
        )

    def vel_copy(d, slot):
        return pltpu.make_async_remote_copy(
            src_ref=vel_t.at[:, pl.ds(0, tpd)],
            dst_ref=vel_t.at[:, pl.ds((1 + slot) * tpd, tpd)],
            send_sem=face_send.at[SWEEPS, d],
            recv_sem=face_recv.at[SWEEPS, slot],
            device_id=at(FACES[d]),
            device_id_type=MESH,
        )

    def p_copy(s):
        def make(d, slot):
            return pltpu.make_async_remote_copy(
                src_ref=p_t.at[s, pl.ds(0, tpd)],
                dst_ref=p_t.at[s, pl.ds((1 + slot) * tpd, tpd)],
                send_sem=face_send.at[s, d],
                recv_sem=face_recv.at[s, slot],
                device_id=at(FACES[d]),
                device_id_type=MESH,
            )

        return make

    def start_faces(make):
        for d in range(6):

            @pl.when(inside(FACES[d]))
            def _(d=d):
                make(d, d ^ 1).start()

    def recv_faces(make):
        for d in range(6):

            @pl.when(inside(FACES[d]))
            def _(d=d):
                make(d, d).wait_recv()

    def sent_faces(make):
        for d in range(6):

            @pl.when(inside(FACES[d]))
            def _(d=d):
                make(d, d ^ 1).wait_send()

    for number, rel in enumerate(OFFSETS):

        @pl.when(inside(rel))
        def _(number=number):
            part_copy(number).start()

    start_faces(lin_copy)

    def hot_of(ref, rows):
        slots = ref[pl.ds(QROWS, rows, stride=BLOCK), :]
        lane = lax.broadcasted_iota(jnp.int32, (rows, LANES), 1).astype(jnp.float32)
        return jnp.where(slots == lane, 1.0, 0.0)

    own_hot = jnp.transpose(hot_of(parts, SELF_BINS))[0:tpd].astype(jnp.bfloat16)
    own = [
        pick(own_hot, parts[pl.ds(r, SELF_BINS, stride=BLOCK), :]) for r in range(QROWS)
    ]
    for number, rel in enumerate(OFFSETS):

        @pl.when(inside(neg(rel)))
        def _(number=number):
            part_copy(number).wait_recv()

    near_hot_t = hot_of(got, near_pad)
    near_hot = jnp.transpose(near_hot_t)[0:tpd].astype(jnp.bfloat16)
    pieces = [
        own[r] + pick(near_hot, got[pl.ds(r, near_pad, stride=BLOCK), :]) for r in range(QROWS)
    ]
    totals = [
        jnp.concatenate(pieces[q * GROUPS : (q + 1) * GROUPS], axis=1) for q in range(4)
    ]
    fluid = totals[0] > 0.0
    safe = jnp.where(fluid, totals[0], 1.0)
    vel = [jnp.where(fluid, totals[1 + a] / safe, 0.0) for a in range(3)]
    vel[1] = vel[1] - GRAVITY * jnp.where(fluid, 1.0, 0.0)
    for a in range(3):
        vel_t[a, 0:tpd, :] = vel[a]
    start_faces(vel_copy)

    recv_faces(lin_copy)
    lane = lax.broadcasted_iota(jnp.int32, (8, LANES), 1) // tpd
    cand = jnp.where(lane == 0, lin_row[...], -1)
    for d in range(6):
        cand = jnp.where(lane == d + 1, lins[d], cand)
    here = lin_col[...]
    hots = []
    for face in FACES:
        delta = (face[0] * 1024 + face[1]) * 1024 + face[2]
        hots.append(jnp.where(cand[0:1] == here + delta, 1.0, 0.0))

    recv_faces(vel_copy)
    div = None
    for a in range(3):
        hot = jnp.concatenate(hots[2 * a : 2 * a + 2], axis=0).astype(jnp.bfloat16)
        ghost = pick(hot, vel_t[a])
        term = 0.5 * (
            shifted(vel[a], ghost[0:tpd], 2 * a) - shifted(vel[a], ghost[tpd:], 2 * a + 1)
        )
        div = term if div is None else div + term

    all_hot = jnp.concatenate(hots, axis=0).astype(jnp.bfloat16)
    press = jnp.where(fluid, (0.0 - div) / 6.0, 0.0)
    for s in range(SWEEPS):
        p_t[s, 0:tpd, :] = press
        start_faces(p_copy(s))
        recv_faces(p_copy(s))
        ghost = pick(all_hot, p_t[s])
        sides = [
            shifted(press, ghost[d * tpd : (d + 1) * tpd], d) for d in range(6)
        ]
        if s < SWEEPS - 1:
            total = sides[0]
            for d in range(1, 6):
                total = total + sides[d]
            press = jnp.where(fluid, (total - div) / 6.0, 0.0)
    out_p[...] = press
    near_rows = near_hot_t[:, 0:tpd].astype(jnp.bfloat16)
    for a in range(3):
        v = jnp.where(fluid, vel[a] - 0.5 * (sides[2 * a] - sides[2 * a + 1]), 0.0)
        vel[a] = v
        answer = jnp.dot(near_rows, v.astype(jnp.bfloat16), preferred_element_type=jnp.float32)
        for u in range(GROUPS):
            r = 4 * u + a
            reply[pl.ds(r, near_pad, stride=QROWS), :] = answer[:, u * LANES : (u + 1) * LANES]
    for u in range(GROUPS):
        reply[pl.ds(4 * u + 3, near_pad, stride=QROWS), :] = jnp.zeros(
            (near_pad, LANES), jnp.float32
        )
    for number, rel in enumerate(OFFSETS):

        @pl.when(inside(neg(rel)))
        def _(number=number):
            reply_copy(number).start()

    for a in range(3):
        out_vel[a] = vel[a]
        for u in range(GROUPS):
            out_table[pl.ds(4 * u + a, tpd, stride=QROWS), :] = vel[a][
                :, u * LANES : (u + 1) * LANES
            ]
    for u in range(GROUPS):
        out_table[pl.ds(4 * u + 3, tpd, stride=QROWS), :] = jnp.zeros((tpd, LANES), jnp.float32)

    for number, rel in enumerate(OFFSETS):

        @pl.when(inside(rel))
        def _(number=number):
            part_copy(number).wait_send()

    sent_faces(lin_copy)
    sent_faces(vel_copy)
    for s in range(SWEEPS):
        sent_faces(p_copy(s))
    for number, rel in enumerate(OFFSETS):

        @pl.when(inside(rel))
        def _(number=number):
            reply_copy(number).wait_recv()

        @pl.when(inside(neg(rel)))
        def _(number=number):
            reply_copy(number).wait_send()

    near_rows_all = len(OFFSETS) * per * QROWS
    out_table[pl.ds(tpd * QROWS, near_rows_all), :] = back[...]


def local(
    sizes,
    tile_coords,
    owner_map,
    bin_tile,
    bin_count,
    part_cell,
    part_offset,
    part_velocity,
    part_affine,
    part_mass,
):
    tpd = tile_coords.shape[1]
    bins, points = part_cell.shape
    near = bins - SELF_BINS
    per = near // len(OFFSETS)
    near_pad = -(-near // 8) * 8
    steps = -(-bins // STEP_BINS)
    f32 = jnp.float32

    def rows(i, *_):
        return (i, 0)

    def slabs(i, *_):
        return (i, 0, 0)

    parts = pl.pallas_call(
        functools.partial(splat_kernel, bins, tpd),
        out_shape=jax.ShapeDtypeStruct((bins * BLOCK, LANES), f32),
        grid_spec=pltpu.PrefetchScalarGridSpec(
            num_scalar_prefetch=3,
            grid=(steps,),
            in_specs=[
                pl.BlockSpec((STEP_BINS, points), rows),
                pl.BlockSpec((STEP_BINS, 3, points), slabs),
                pl.BlockSpec((STEP_BINS, 3, points), slabs),
                pl.BlockSpec((STEP_BINS, 9, points), slabs),
                pl.BlockSpec((STEP_BINS, points), rows),
            ],
            out_specs=pl.BlockSpec((STEP_BINS * BLOCK, LANES), rows),
        ),
        compiler_params=pltpu.CompilerParams(dimension_semantics=("arbitrary",)),
        name="splat",
    )(owner_map, bin_tile, bin_count, part_cell, part_offset, part_velocity, part_affine, part_mass)

    lin = (tile_coords[0] * 1024 + tile_coords[1]) * 1024 + tile_coords[2]
    lin_row = jnp.broadcast_to(jnp.tile(lin, LANES // tpd)[None, :], (8, LANES))
    lin_col = jnp.broadcast_to(lin[:, None], (tpd, LANES))
    vmem = pl.BlockSpec(memory_space=pltpu.VMEM)
    dma = pltpu.SemaphoreType.DMA
    count = len(OFFSETS)
    velocity, pressure, table = pl.pallas_call(
        functools.partial(grid_kernel, sizes, tpd, per, near_pad),
        out_shape=(
            jax.ShapeDtypeStruct((3, tpd, CELLS), f32),
            jax.ShapeDtypeStruct((tpd, CELLS), f32),
            jax.ShapeDtypeStruct(((tpd + near) * QROWS, LANES), f32),
        ),
        in_specs=[vmem] * 3,
        out_specs=(vmem, vmem, vmem),
        scratch_shapes=[
            pltpu.VMEM((6, 8, LANES), jnp.int32),
            pltpu.VMEM((near_pad * BLOCK, LANES), f32),
            pltpu.VMEM((3, LANES, CELLS), f32),
            pltpu.VMEM((SWEEPS, LANES, CELLS), f32),
            pltpu.VMEM((near_pad * QROWS, LANES), f32),
            pltpu.VMEM((near * QROWS, LANES), f32),
            dma((count,)),
            dma((count,)),
            dma((6,)),
            dma((6,)),
            dma((SWEEPS + 1, 6)),
            dma((SWEEPS + 1, 6)),
            dma((count,)),
            dma((count,)),
        ],
        compiler_params=pltpu.CompilerParams(collective_id=0, has_side_effects=True),
        name="grid",
    )(lin_row, lin_col, parts)

    sampled = pl.pallas_call(
        functools.partial(sample_kernel, bins, tpd),
        out_shape=jax.ShapeDtypeStruct((bins, 3, points), f32),
        grid_spec=pltpu.PrefetchScalarGridSpec(
            num_scalar_prefetch=3,
            grid=(steps,),
            in_specs=[
                pl.BlockSpec((STEP_BINS, points), rows),
                pl.BlockSpec(((tpd + near) * QROWS, LANES), lambda i, *_: (0, 0)),
            ],
            out_specs=pl.BlockSpec((STEP_BINS, 3, points), slabs),
        ),
        compiler_params=pltpu.CompilerParams(dimension_semantics=("arbitrary",)),
        name="sample",
    )(owner_map, bin_tile, bin_count, part_cell, table)
    return velocity.reshape(3, tpd * CELLS), pressure.reshape(-1), sampled


def solution(mesh):
    split_all = AXES
    placed = (
        P(None, split_all),
        P(),
        P(split_all),
        P(split_all),
        P(split_all, None),
        P(split_all, None, None),
        P(split_all, None, None),
        P(split_all, None, None),
        P(split_all, None),
    )
    sizes = tuple(mesh.shape[name] for name in AXES)
    return jax.shard_map(
        functools.partial(local, sizes),
        mesh=mesh,
        in_specs=placed,
        out_specs=(P(None, split_all), P(split_all), P(split_all, None, None)),
        check_vma=False,
    )
```

time: 596 us -> 86.7 us (0.15); the launches traced: 585 us -> 86.3 us
  local copies, waits for them, and re-layouts: 330 us -> 19.7 us
  starting transfers between devices: 109 us -> 0 us
  waiting for transfers between devices: 75.3 us -> 0 us
  Pallas kernels: 0 us -> 65.2 us
  other arithmetic: 42.8 us -> 0.84 us
  matrix products: 24.6 us -> 0 us
    gather x31 -> x0, local copies, waits for them, and re-layouts: 140 us -> none  [the longest x30 139 us: beside(): face_table[jnp.maximum(chosen_rows, 0), facing]]
    ppermute x54 -> x0, starting transfers between devices: 109 us -> none  [the longest x18 44.2 us: with_halo(): lax.ppermute(lax.slice_in_dim(block, block.shape[dim] - width, None, axis...]
    ppermute x54 -> x0, waiting for transfers between devices: 75.3 us -> none  [the longest x18 54.9 us: with_halo(): lax.ppermute(lax.slice_in_dim(block, 0, width, axis=dim), axis, backward)]
    pallas_call x0 -> x3, Pallas kernels: none -> 65.2 us  [the longest x1 40.5 us: local(): pl.pallas_call(functools.partial(grid_kernel, sizes, tpd, per, near_pad),...]
    reshape x33 -> x0, local copies, waits for them, and re-layouts: 51.1 us -> none  [the longest x8 36.4 us: pressure_table(): return gathered.reshape(27 * TPD, 6, TILE, TILE)]
    eq x48 -> x0, local copies, waits for them, and re-layouts: 31.8 us -> none  [the longest x29 21.4 us: splat_block(): lower_block[:, :, None]]
    dot_general x50 -> x0, matrix products: 24.6 us -> none  [the longest x17 13.9 us: sample_block(): jnp.einsum('gul,glp->gup', tile_block.reshape(group_size, 3 * TILE, plane...]
    concatenate x19 -> x0, local copies, waits for them, and re-layouts: 22.9 us -> none  [the longest x10 16.7 us: stack_rows(): jnp.concatenate([portion[member] for portion in pieces], axis=0)]
  transfers between devices with their start and end apart: 54 -> 0, of which waited for: 33 -> 0; matrix products, arithmetic and copies ran while one was open for 24% -> 0% of each run, Pallas kernels for 0% -> 0%
where the time goes in v1:
time: 86.7 us; the launch traced here: 86.3 us
  Pallas kernels  65.2 us (75%)
  local copies, waits for them, and re-layouts  19.7 us (23%)
    pallas_call x1, Pallas kernels, local(): pl.pallas_call(functools.partial(grid_kernel, sizes, tpd, per, near_pad),...  40.5 us
    unnamed x10, local copies, waits for them, and re-layouts  18.3 us
    pallas_call x1, Pallas kernels, local(): pl.pallas_call(functools.partial(splat_kernel, bins, tpd), out_shape=jax....  14.4 us
    pallas_call x1, Pallas kernels, local(): pl.pallas_call(functools.partial(sample_kernel, bins, tpd), out_shape=jax...  10.3 us

profile of v1, /device:TPU:0, one launch (start us, length us, event | category | flops | bytes accessed | tf_op | source)
XLA Modules:
  0.0 86.3 jit_solution(2760313139707569387)
XLA Ops:
  0.6 0.0 copy-start.1
  0.6 0.8 add_bitcast_fusion
  1.5 0.1 broadcast_in_dim.6
  1.6 0.6 broadcast_in_dim.14.lin_row
  2.2 0.7 broadcast_in_dim.15.lin_col
  2.8 0.0 copy-start
  2.8 3.9 %copy.12.offset = f32[58,3,2048]{2,1,0:T(4,128)} copy(f32[58,3,2048]{2,0,1:T(8,128)} %param.14) | data formatting | bytes 2850816 | tf_op args[5]
  6.7 0.0 copy-done.1
  6.7 2.2 %copy.13.velocity = f32[58,3,2048]{2,1,0:T(4,128)} copy(f32[58,3,2048]{2,0,1:T(8,128)S(1)} %copy-done.1) | data formatting | bytes 2850816 | tf_op args[6]
  8.9 0.0 copy-done
  8.9 5.7 %copy.14.affine = f32[58,9,2048]{2,1,0:T(8,128)} copy(f32[58,9,2048]{2,0,1:T(8,128)S(1)} %copy-done) | data formatting | bytes 8552448 | tf_op args[7]
  14.7 14.4 %splat.1.parts = f32[1392,128]{1,0:T(8,128)} custom-call(s32[512]{0:T(512)} %owner.3, s32[58]{0:T(128)} %tile.13, s32[58]{0:T(128)} %count.3, s32[58,2048]{1,0:T(8,128)} %cell.3, f32[58,3,2048]{2,1,0:T(4,128)} %copy.12.offset, f32[58,3,2048]{2,1,0:T(4,128)} %copy.13.velocity, f32[58,9,2048]{2,1,0:T(8,128)} %copy.14.affine, f32[58,2048]{1,0:T(8,128)} %mass.1), custom_call_target="tpu_custom_call" | custom-call | tf_op jit(solution)/shard_map/splat/pallas_call | solution.py:440
  29.1 40.5 %grid.1 = (f32[3,16,512]{2,1,0:T(8,128)}, f32[16,512]{1,0:T(8,128)}, f32[672,128]{1,0:T(8,128)}) custom-call(s32[8,128]{1,0:T(8,128)} %broadcast_in_dim.14.lin_row, s32[16,128]{1,0:T(8,128)} %broadcast_in_dim.15.lin_col, f32[1392,128]{1,0:T(8,128)} %splat.1.parts), custom_call_target="tpu_custom_call" | custom-call | tf_op jit(solution)/shard_map/grid/pallas_call | solution.py:465
  69.6 1.4 %copy.17 = f32[2,4,8,128]{3,1,2,0:T(4,128)} copy(f32[2,4,8,128]{3,2,1,0:T(8,128)} %bitcast.9) | data formatting | bytes 65536
  71.0 1.6 %copy.16 = f32[1,3,16,512]{3,1,2,0:T(4,128)} copy(f32[1,3,16,512]{3,2,1,0:T(8,128)} %bitcast.7) | data formatting | bytes 196608
  72.6 10.3 %sample.1 = f32[58,3,2048]{2,1,0:T(4,128)} custom-call(s32[512]{0:T(512)} %owner.3, s32[58]{0:T(128)} %tile.13, s32[58]{0:T(128)} %count.3, s32[58,2048]{1,0:T(8,128)} %cell.3, f32[672,128]{1,0:T(8,128)} %get-tuple-element.8.table), custom_call_target="tpu_custom_call" | custom-call | tf_op jit(solution)/shard_map/sample/pallas_call | solution.py:494
  82.9 3.5 %copy.15 = f32[58,3,2048]{2,0,1:T(8,128)} copy(f32[58,3,2048]{2,1,0:T(4,128)} %sample.1) | data formatting | bytes 2850816
  (1 shorter events, 0.0 us)
Async XLA Ops:
  0.6 6.1 %copy-start.1 = (f32[58,3,2048]{2,0,1:T(8,128)S(1)}, f32[58,3,2048]{2,0,1:T(8,128)}, u32[]{:S(2)}) copy-start(f32[58,3,2048]{2,0,1:T(8,128)} %param.15) | copy-start | bytes 4276228
  2.8 6.1 %copy-start = (f32[58,9,2048]{2,0,1:T(8,128)S(1)}, f32[58,9,2048]{2,0,1:T(8,128)}, u32[]{:S(2)}) copy-start(f32[58,9,2048]{2,0,1:T(8,128)} %param.16) | copy-start | bytes 12828676

commit v2 on v1

--- a/solution.py
+++ b/solution.py
@@ -56,28 +56,28 @@
 
 
 def splat_kernel(
-    bins, slots_of, owner, tile, count, cell, offset, velocity, affine, mass, out
+    bins, slots_of, owner, tile, count, cell, offset, velocity, affine, mass, out, dep
 ):
     step = pl.program_id(0)
+    points = cell.shape[1]
+    m = mass[...]
+    dep[0] = m
+    for a in range(3):
+        drift = affine[3 * a] * offset[0]
+        for e in (1, 2):
+            drift = drift + affine[3 * a + e] * offset[e]
+        dep[a + 1] = m * (velocity[a] - drift)
 
     def one(j):
         b = step * STEP_BINS + j
-        points = cell.shape[1]
         cells = cell[pl.ds(j, 1), :]
-        m = mass[pl.ds(j, 1), :]
-        moved = []
-        for a in range(3):
-            drift = affine[j, pl.ds(3 * a, 1), :] * offset[j, pl.ds(0, 1), :]
-            for e in (1, 2):
-                drift = drift + affine[j, pl.ds(3 * a + e, 1), :] * offset[j, pl.ds(e, 1), :]
-            moved.append(m * (velocity[j, pl.ds(a, 1), :] - drift))
         upper = upper_row(cells, count[b])
         sub = lax.broadcasted_iota(jnp.int32, (8, points), 0)
         hit = (sub & 3) == upper
         first = sub < 4
         halves = []
-        for low, high in ((m, moved[0]), (moved[1], moved[2])):
-            both = jnp.where(first, low, high)
+        for q in (0, 2):
+            both = jnp.where(first, dep[q, pl.ds(j, 1), :], dep[q + 1, pl.ds(j, 1), :])
             halves.append(jnp.where(hit, both, 0.0))
         weighted = jnp.concatenate(halves, axis=0).astype(jnp.bfloat16)
         summed = lax.dot_general(
@@ -112,7 +112,9 @@
         val = jnp.where(upper == half, planes[0:8], 0.0)
         for k in range(1, GROUPS // 2):
             val = val + jnp.where(upper == half + 2 * k, planes[8 * k : 8 * k + 8], 0.0)
-        out[j] = val[0:3] + val[4:7]
+        val = val[0:4] + val[4:8]
+        for a in range(3):
+            out[a, pl.ds(j, 1), :] = val[a : a + 1]
 
     bins_of_step(step, bins, one)
 
@@ -149,12 +151,12 @@
     tpd,
     per,
     near_pad,
-    lin_row,
-    lin_col,
+    coords,
     parts,
     out_vel,
     out_p,
     out_table,
+    lin_row,
     lins,
     got,
     vel_t,
@@ -189,7 +191,11 @@
     def neg(rel):
         return tuple(-v for v in rel)
 
-    lins[...] = jnp.full(lins.shape, -1, jnp.int32)
+    lin = (coords[0:1] * 64 + coords[1:2]) * 64 + coords[2:3]
+    lin = jnp.concatenate([lin.astype(jnp.float32)] * (LANES // tpd), axis=1)
+    lin_row[...] = jnp.broadcast_to(lin, (8, LANES))
+    here = jnp.transpose(jnp.broadcast_to(lin, (LANES, LANES)))[0:tpd]
+    lins[...] = jnp.full(lins.shape, -1.0, jnp.float32)
     got[...] = jnp.zeros(got.shape, jnp.float32)
     vel_t[...] = jnp.zeros(vel_t.shape, jnp.float32)
     p_t[...] = jnp.zeros(p_t.shape, jnp.float32)
@@ -325,13 +331,12 @@
 
     recv_faces(lin_copy)
     lane = lax.broadcasted_iota(jnp.int32, (8, LANES), 1) // tpd
-    cand = jnp.where(lane == 0, lin_row[...], -1)
+    cand = jnp.where(lane == 0, lin_row[...], -1.0)
     for d in range(6):
         cand = jnp.where(lane == d + 1, lins[d], cand)
-    here = lin_col[...]
     hots = []
     for face in FACES:
-        delta = (face[0] * 1024 + face[1]) * 1024 + face[2]
+        delta = float((face[0] * 64 + face[1]) * 64 + face[2])
         hots.append(jnp.where(cand[0:1] == here + delta, 1.0, 0.0))
 
     recv_faces(vel_copy)
@@ -359,7 +364,8 @@
             for d in range(1, 6):
                 total = total + sides[d]
             press = jnp.where(fluid, (total - div) / 6.0, 0.0)
-    out_p[...] = press
+    for u in range(GROUPS):
+        out_p[pl.ds(u, tpd, stride=GROUPS), :] = press[:, u * LANES : (u + 1) * LANES]
     near_rows = near_hot_t[:, 0:tpd].astype(jnp.bfloat16)
     for a in range(3):
         v = jnp.where(fluid, vel[a] - 0.5 * (sides[2 * a] - sides[2 * a + 1]), 0.0)
@@ -379,7 +385,8 @@
             reply_copy(number).start()
 
     for a in range(3):
-        out_vel[a] = vel[a]
+        for t in range(tpd):
+            out_vel[a : a + 1, t * CELLS : (t + 1) * CELLS] = vel[a][t : t + 1]
         for u in range(GROUPS):
             out_table[pl.ds(4 * u + a, tpd, stride=QROWS), :] = vel[a][
                 :, u * LANES : (u + 1) * LANES
@@ -435,8 +442,11 @@
         return (i, 0)
 
     def slabs(i, *_):
-        return (i, 0, 0)
-
+        return (0, i, 0)
+
+    by_component = [
+        jnp.transpose(x, (1, 0, 2)) for x in (part_offset, part_velocity, part_affine)
+    ]
     parts = pl.pallas_call(
         functools.partial(splat_kernel, bins, tpd),
         out_shape=jax.ShapeDtypeStruct((bins * BLOCK, LANES), f32),
@@ -445,34 +455,33 @@
             grid=(steps,),
             in_specs=[
                 pl.BlockSpec((STEP_BINS, points), rows),
-                pl.BlockSpec((STEP_BINS, 3, points), slabs),
-                pl.BlockSpec((STEP_BINS, 3, points), slabs),
-                pl.BlockSpec((STEP_BINS, 9, points), slabs),
+                pl.BlockSpec((3, STEP_BINS, points), slabs),
+                pl.BlockSpec((3, STEP_BINS, points), slabs),
+                pl.BlockSpec((9, STEP_BINS, points), slabs),
                 pl.BlockSpec((STEP_BINS, points), rows),
             ],
             out_specs=pl.BlockSpec((STEP_BINS * BLOCK, LANES), rows),
+            scratch_shapes=[pltpu.VMEM((4, STEP_BINS, points), f32)],
         ),
         compiler_params=pltpu.CompilerParams(dimension_semantics=("arbitrary",)),
         name="splat",
-    )(owner_map, bin_tile, bin_count, part_cell, part_offset, part_velocity, part_affine, part_mass)
-
-    lin = (tile_coords[0] * 1024 + tile_coords[1]) * 1024 + tile_coords[2]
-    lin_row = jnp.broadcast_to(jnp.tile(lin, LANES // tpd)[None, :], (8, LANES))
-    lin_col = jnp.broadcast_to(lin[:, None], (tpd, LANES))
+    )(owner_map, bin_tile, bin_count, part_cell, *by_component, part_mass)
+
     vmem = pl.BlockSpec(memory_space=pltpu.VMEM)
     dma = pltpu.SemaphoreType.DMA
     count = len(OFFSETS)
     velocity, pressure, table = pl.pallas_call(
         functools.partial(grid_kernel, sizes, tpd, per, near_pad),
         out_shape=(
-            jax.ShapeDtypeStruct((3, tpd, CELLS), f32),
-            jax.ShapeDtypeStruct((tpd, CELLS), f32),
+            jax.ShapeDtypeStruct((3, tpd * CELLS), f32),
+            jax.ShapeDtypeStruct((tpd * GROUPS, LANES), f32),
             jax.ShapeDtypeStruct(((tpd + near) * QROWS, LANES), f32),
         ),
-        in_specs=[vmem] * 3,
+        in_specs=[vmem] * 2,
         out_specs=(vmem, vmem, vmem),
         scratch_shapes=[
-            pltpu.VMEM((6, 8, LANES), jnp.int32),
+            pltpu.VMEM((8, LANES), f32),
+            pltpu.VMEM((6, 8, LANES), f32),
             pltpu.VMEM((near_pad * BLOCK, LANES), f32),
             pltpu.VMEM((3, LANES, CELLS), f32),
             pltpu.VMEM((SWEEPS, LANES, CELLS), f32),
@@ -489,11 +498,11 @@
         ],
         compiler_params=pltpu.CompilerParams(collective_id=0, has_side_effects=True),
         name="grid",
-    )(lin_row, lin_col, parts)
+    )(tile_coords, parts)
 
     sampled = pl.pallas_call(
         functools.partial(sample_kernel, bins, tpd),
-        out_shape=jax.ShapeDtypeStruct((bins, 3, points), f32),
+        out_shape=jax.ShapeDtypeStruct((3, bins, points), f32),
         grid_spec=pltpu.PrefetchScalarGridSpec(
             num_scalar_prefetch=3,
             grid=(steps,),
@@ -501,12 +510,12 @@
                 pl.BlockSpec((STEP_BINS, points), rows),
                 pl.BlockSpec(((tpd + near) * QROWS, LANES), lambda i, *_: (0, 0)),
             ],
-            out_specs=pl.BlockSpec((STEP_BINS, 3, points), slabs),
+            out_specs=pl.BlockSpec((3, STEP_BINS, points), slabs),
         ),
         compiler_params=pltpu.CompilerParams(dimension_semantics=("arbitrary",)),
         name="sample",
     )(owner_map, bin_tile, bin_count, part_cell, table)
-    return velocity.reshape(3, tpd * CELLS), pressure.reshape(-1), sampled
+    return velocity, pressure.reshape(-1), jnp.transpose(sampled, (1, 0, 2))
 
 
 def solution(mesh):

time: 86.7 us -> 68 us (0.78)
  local copies, waits for them, and re-layouts: 19.7 us -> 1.28 us
    unnamed x10 -> x6, local copies, waits for them, and re-layouts: 18.3 us -> 1.28 us
    broadcast_in_dim x3 -> x0, local copies, waits for them, and re-layouts: 1.35 us -> none  [the longest x2 0.68 us: local(): lin_row = jnp.broadcast_to(jnp.tile(lin, LANES // tpd)[None, :], (8, LANES))]
where the time goes in v2:
time: 68 us; the launch traced here: 67.7 us
  Pallas kernels  65.8 us (97%)
  local copies, waits for them, and re-layouts  1.28 us (2%)
    pallas_call x1, Pallas kernels, local(): pl.pallas_call(functools.partial(grid_kernel, sizes, tpd, per, near_pad),...  40.5 us
    pallas_call x1, Pallas kernels, local(): pl.pallas_call(functools.partial(splat_kernel, bins, tpd), out_shape=jax....  14.7 us
    pallas_call x1, Pallas kernels, local(): pl.pallas_call(functools.partial(sample_kernel, bins, tpd), out_shape=jax...  10.6 us

profile of v2, /device:TPU:0, one launch (start us, length us, event | category | flops | bytes accessed | tf_op | source)
XLA Modules:
  0.0 67.7 jit_solution(14296983307742376312)
XLA Ops:
  0.6 14.7 %splat.1.parts = f32[1392,128]{1,0:T(8,128)} custom-call(s32[512]{0:T(512)} %owner.3, s32[58]{0:T(128)} %tile.3, s32[58]{0:T(128)} %count.3, s32[58,2048]{1,0:T(8,128)} %cell.3, f32[3,58,2048]{2,1,0:T(8,128)} %bitcast.6, f32[3,58,2048]{2,1,0:T(8,128)} %bitcast.7, f32[9,58,2048]{2,1,0:T(8,128)} %bitcast.5, f32[58,2048]{1,0:T(8,128)} %mass.1), custom_call_target="tpu_custom_call" | custom-call | tf_op jit(solution)/shard_map/splat/pallas_call | solution.py:450
  15.3 40.5 %grid.1 = (f32[3,8192]{1,0:T(4,128)}, f32[64,128]{1,0:T(8,128)}, f32[672,128]{1,0:T(8,128)}) custom-call(s32[3,16]{1,0:T(4,128)} %coords.1, f32[1392,128]{1,0:T(8,128)} %splat.1.parts), custom_call_target="tpu_custom_call" | custom-call | tf_op jit(solution)/shard_map/grid/pallas_call | solution.py:473
  55.8 0.0 copy-start
  55.8 0.0 copy-start.1
  55.8 10.6 %sample.1 = f32[3,58,2048]{2,1,0:T(8,128)} custom-call(s32[512]{0:T(512)} %owner.3, s32[58]{0:T(128)} %tile.3, s32[58]{0:T(128)} %count.3, s32[58,2048]{1,0:T(8,128)} %cell.3, f32[672,128]{1,0:T(8,128)} %get-tuple-element.8.table), custom_call_target="tpu_custom_call" | custom-call | tf_op jit(solution)/shard_map/sample/pallas_call | solution.py:503
  66.5 0.0 copy-done
  66.5 0.7 copy.14
  67.1 0.0 copy-done.1
  67.1 0.6 copy.15
Async XLA Ops:
  55.8 10.7 %copy-start = (f32[3,8192]{1,0:T(4,128)S(1)}, f32[3,8192]{1,0:T(4,128)}, u32[]{:S(2)}) copy-start(f32[3,8192]{1,0:T(4,128)} %get-tuple-element.12) | copy-start | bytes 294916
  55.8 11.3 %copy-start.1 = (f32[64,128]{1,0:T(8,128)S(1)}, f32[64,128]{1,0:T(8,128)}, u32[]{:S(2)}) copy-start(f32[64,128]{1,0:T(8,128)} %get-tuple-element.7) | copy-start | bytes 98308

commit v3 on v2

--- a/solution.py
+++ b/solution.py
@@ -132,18 +132,41 @@
     )
 
 
+def tile_of(x, u):
+    return x[:, u * LANES : (u + 1) * LANES]
+
+
+def pack_faces(field, axis):
+    lane = lax.broadcasted_iota(jnp.int32, (field.shape[0], LANES), 1)
+    half = TILE * TILE
+    if axis == 0:
+        both = jnp.where(lane < half, tile_of(field, 0), tile_of(field, GROUPS - 1))
+        return pltpu.roll(both, half, 1)
+    stride = (TILE, 1)[axis - 1]
+    pos = (lane // stride) % TILE
+    packed = jnp.zeros((field.shape[0], LANES), jnp.float32)
+    for u in range(GROUPS):
+        low = (TILE - 1 - u) * stride
+        piece = tile_of(field, u)
+        packed = jnp.where(pos == TILE - 1 - u, pltpu.roll(piece, low, 1), packed)
+        packed = jnp.where(pos == u, pltpu.roll(piece, LANES - low, 1), packed)
+    return packed
+
+
 def shifted(field, ghost, facing):
     lane = lax.broadcasted_iota(jnp.int32, field.shape, 1)
     stride = (TILE * TILE, TILE, 1)[facing // 2]
     pos = (lane // stride) % TILE
-    wrap = stride * (TILE - 1)
+    outer = []
+    for u in range(GROUPS):
+        move = 0 if facing < 2 else u * stride
+        if move and facing % 2:
+            move = LANES - move
+        outer.append(pltpu.roll(ghost, move, 1) if move else ghost)
+    outer = jnp.concatenate(outer, axis=1)
     if facing % 2 == 0:
-        inner = pltpu.roll(field, CELLS - stride, 1)
-        outer = pltpu.roll(ghost, wrap, 1)
-        return jnp.where(pos == TILE - 1, outer, inner)
-    inner = pltpu.roll(field, stride, 1)
-    outer = pltpu.roll(ghost, CELLS - wrap, 1)
-    return jnp.where(pos == 0, outer, inner)
+        return jnp.where(pos == TILE - 1, outer, pltpu.roll(field, CELLS - stride, 1))
+    return jnp.where(pos == 0, outer, pltpu.roll(field, stride, 1))
 
 
 def grid_kernel(
@@ -215,10 +238,11 @@
     pl.semaphore_wait(barrier, spans[0] * spans[1] * spans[2] - 1)
 
     def part_copy(number):
-        rows = per * BLOCK
+        start = number * per * BLOCK
+        rows = (per - 1) * BLOCK + QROWS + 1
         return pltpu.make_async_remote_copy(
-            src_ref=parts.at[pl.ds(SELF_BINS * BLOCK + number * rows, rows)],
-            dst_ref=got.at[pl.ds(number * rows, rows)],
+            src_ref=parts.at[pl.ds(SELF_BINS * BLOCK + start, rows)],
+            dst_ref=got.at[pl.ds(start, rows)],
             send_sem=part_send.at[number],
             recv_sem=part_recv.at[number],
             device_id=at(OFFSETS[number]),
@@ -248,8 +272,8 @@
 
     def vel_copy(d, slot):
         return pltpu.make_async_remote_copy(
-            src_ref=vel_t.at[:, pl.ds(0, tpd)],
-            dst_ref=vel_t.at[:, pl.ds((1 + slot) * tpd, tpd)],
+            src_ref=vel_t.at[pl.ds(0, tpd)],
+            dst_ref=vel_t.at[pl.ds((1 + slot) * tpd, tpd)],
             send_sem=face_send.at[SWEEPS, d],
             recv_sem=face_recv.at[SWEEPS, slot],
             device_id=at(FACES[d]),
@@ -326,7 +350,7 @@
     vel = [jnp.where(fluid, totals[1 + a] / safe, 0.0) for a in range(3)]
     vel[1] = vel[1] - GRAVITY * jnp.where(fluid, 1.0, 0.0)
     for a in range(3):
-        vel_t[a, 0:tpd, :] = vel[a]
+        vel_t[0:tpd, a * LANES : (a + 1) * LANES] = pack_faces(vel[a], a)
     start_faces(vel_copy)
 
     recv_faces(lin_copy)
@@ -339,26 +363,29 @@
         delta = float((face[0] * 64 + face[1]) * 64 + face[2])
         hots.append(jnp.where(cand[0:1] == here + delta, 1.0, 0.0))
 
+    pair_hots = [
+        jnp.concatenate(hots[2 * a : 2 * a + 2], axis=0).astype(jnp.bfloat16) for a in range(3)
+    ]
     recv_faces(vel_copy)
     div = None
     for a in range(3):
-        hot = jnp.concatenate(hots[2 * a : 2 * a + 2], axis=0).astype(jnp.bfloat16)
-        ghost = pick(hot, vel_t[a])
+        ghost = pick(pair_hots[a], vel_t[:, a * LANES : (a + 1) * LANES])
         term = 0.5 * (
             shifted(vel[a], ghost[0:tpd], 2 * a) - shifted(vel[a], ghost[tpd:], 2 * a + 1)
         )
         div = term if div is None else div + term
 
-    all_hot = jnp.concatenate(hots, axis=0).astype(jnp.bfloat16)
     press = jnp.where(fluid, (0.0 - div) / 6.0, 0.0)
     for s in range(SWEEPS):
-        p_t[s, 0:tpd, :] = press
+        for a in range(3):
+            p_t[s, 0:tpd, a * LANES : (a + 1) * LANES] = pack_faces(press, a)
         start_faces(p_copy(s))
         recv_faces(p_copy(s))
-        ghost = pick(all_hot, p_t[s])
-        sides = [
-            shifted(press, ghost[d * tpd : (d + 1) * tpd], d) for d in range(6)
-        ]
+        sides = []
+        for a in range(3):
+            ghost = pick(pair_hots[a], p_t[s, :, a * LANES : (a + 1) * LANES])
+            sides.append(shifted(press, ghost[0:tpd], 2 * a))
+            sides.append(shifted(press, ghost[tpd:], 2 * a + 1))
         if s < SWEEPS - 1:
             total = sides[0]
             for d in range(1, 6):
@@ -483,8 +510,8 @@
             pltpu.VMEM((8, LANES), f32),
             pltpu.VMEM((6, 8, LANES), f32),
             pltpu.VMEM((near_pad * BLOCK, LANES), f32),
-            pltpu.VMEM((3, LANES, CELLS), f32),
-            pltpu.VMEM((SWEEPS, LANES, CELLS), f32),
+            pltpu.VMEM((LANES, 3 * LANES), f32),
+            pltpu.VMEM((SWEEPS, LANES, 3 * LANES), f32),
             pltpu.VMEM((near_pad * QROWS, LANES), f32),
             pltpu.VMEM((near * QROWS, LANES), f32),
             dma((count,)),

time: 68 us -> 63.6 us (0.935)
  Pallas kernels: 65.8 us -> 61.4 us
    pallas_call x1, Pallas kernels: 40.5 us -> 36.1 us  [local(): pl.pallas_call(functools.partial(grid_kernel, sizes, tpd, per, near_pad),...]
where the time goes in v3:
time: 63.6 us; the launch traced here: 63.4 us
  Pallas kernels  61.4 us (97%)
  local copies, waits for them, and re-layouts  1.28 us (2%)
  between operations  0.66 us (1%)
    pallas_call x1, Pallas kernels, local(): pl.pallas_call(functools.partial(grid_kernel, sizes, tpd, per, near_pad),...  36.1 us
    pallas_call x1, Pallas kernels, local(): pl.pallas_call(functools.partial(splat_kernel, bins, tpd), out_shape=jax....  14.7 us
    pallas_call x1, Pallas kernels, local(): pl.pallas_call(functools.partial(sample_kernel, bins, tpd), out_shape=jax...  10.6 us
    unnamed x6, local copies, waits for them, and re-layouts  1.28 us

profile of v3, /device:TPU:0, one launch (start us, length us, event | category | flops | bytes accessed | tf_op | source)
XLA Modules:
  0.0 63.4 jit_solution(4491534844475672695)
XLA Ops:
  0.6 14.7 %splat.1.parts = f32[1392,128]{1,0:T(8,128)} custom-call(s32[512]{0:T(512)} %owner.3, s32[58]{0:T(128)} %tile.3, s32[58]{0:T(128)} %count.3, s32[58,2048]{1,0:T(8,128)} %cell.3, f32[3,58,2048]{2,1,0:T(8,128)} %bitcast.6, f32[3,58,2048]{2,1,0:T(8,128)} %bitcast.7, f32[9,58,2048]{2,1,0:T(8,128)} %bitcast.5, f32[58,2048]{1,0:T(8,128)} %mass.1), custom_call_target="tpu_custom_call" | custom-call | tf_op jit(solution)/shard_map/splat/pallas_call | solution.py:477
  15.3 36.1 %grid.1 = (f32[3,8192]{1,0:T(4,128)}, f32[64,128]{1,0:T(8,128)}, f32[672,128]{1,0:T(8,128)}) custom-call(s32[3,16]{1,0:T(4,128)} %coords.1, f32[1392,128]{1,0:T(8,128)} %splat.1.parts), custom_call_target="tpu_custom_call" | custom-call | tf_op jit(solution)/shard_map/grid/pallas_call | solution.py:500
  51.4 0.0 copy-start
  51.4 0.0 copy-start.1
  51.4 10.6 %sample.1 = f32[3,58,2048]{2,1,0:T(8,128)} custom-call(s32[512]{0:T(512)} %owner.3, s32[58]{0:T(128)} %tile.3, s32[58]{0:T(128)} %count.3, s32[58,2048]{1,0:T(8,128)} %cell.3, f32[672,128]{1,0:T(8,128)} %get-tuple-element.8.table), custom_call_target="tpu_custom_call" | custom-call | tf_op jit(solution)/shard_map/sample/pallas_call | solution.py:530
  62.1 0.0 copy-done
  62.1 0.7 %copy.14 = f32[3,8192]{1,0:T(4,128)} copy(f32[3,8192]{1,0:T(4,128)S(1)} %copy-done) | data formatting | bytes 196608
  62.7 0.0 copy-done.1
  62.8 0.6 copy.15
Async XLA Ops:
  51.4 10.7 %copy-start = (f32[3,8192]{1,0:T(4,128)S(1)}, f32[3,8192]{1,0:T(4,128)}, u32[]{:S(2)}) copy-start(f32[3,8192]{1,0:T(4,128)} %get-tuple-element.12) | copy-start | bytes 294916
  51.4 11.3 %copy-start.1 = (f32[64,128]{1,0:T(8,128)S(1)}, f32[64,128]{1,0:T(8,128)}, u32[]{:S(2)}) copy-start(f32[64,128]{1,0:T(8,128)} %get-tuple-element.7) | copy-start | bytes 98308

commit v4 on v3

--- a/solution.py
+++ b/solution.py
@@ -55,22 +55,21 @@
     lax.fori_loop(0, left // unroll, pair, 0)
 
 
-def splat_kernel(
-    bins, slots_of, owner, tile, count, cell, offset, velocity, affine, mass, out, dep
-):
-    step = pl.program_id(0)
+def splat_chunk(start, rows, tpd, owner, tile, count, cell, offset, velocity, affine, mass, out, dep):
     points = cell.shape[1]
-    m = mass[...]
-    dep[0] = m
+    own = pl.ds(start, rows)
+    here = pl.ds(0, rows)
+    m = mass[own, :]
+    dep[0, here, :] = m
     for a in range(3):
-        drift = affine[3 * a] * offset[0]
+        drift = affine[3 * a, own, :] * offset[0, own, :]
         for e in (1, 2):
-            drift = drift + affine[3 * a + e] * offset[e]
-        dep[a + 1] = m * (velocity[a] - drift)
+            drift = drift + affine[3 * a + e, own, :] * offset[e, own, :]
+        dep[a + 1, here, :] = m * (velocity[a, own, :] - drift)
 
     def one(j):
-        b = step * STEP_BINS + j
-        cells = cell[pl.ds(j, 1), :]
+        b = start + j
+        cells = cell[pl.ds(b, 1), :]
         upper = upper_row(cells, count[b])
         sub = lax.broadcasted_iota(jnp.int32, (8, points), 0)
         hit = (sub & 3) == upper
@@ -86,12 +85,19 @@
             (((1,), (1,)), ((), ())),
             preferred_element_type=jnp.float32,
         )
-        base = pl.multiple_of(j * BLOCK, 8)
+        base = pl.multiple_of(b * BLOCK, 8)
         out[pl.ds(base, QROWS), :] = summed
-        slot = lax.rem(owner[tile[b]], slots_of).astype(jnp.float32)
+        slot = lax.rem(owner[tile[b]], tpd).astype(jnp.float32)
         out[pl.ds(base + QROWS, 8), :] = jnp.full((8, LANES), slot, jnp.float32)
 
-    bins_of_step(step, bins, one)
+    unroll = 2 if rows % 2 == 0 else 1
+
+    def pair(i, carry):
+        for k in range(unroll):
+            one(i * unroll + k)
+        return carry
+
+    lax.fori_loop(0, rows // unroll, pair, 0)
 
 
 def sample_kernel(bins, slots_of, owner, tile, count, cell, table, out):
@@ -174,11 +180,26 @@
     tpd,
     per,
     near_pad,
+    owner,
+    tile,
+    count,
     coords,
-    parts,
+    cell_h,
+    offset_h,
+    velocity_h,
+    affine_h,
+    mass_h,
     out_vel,
     out_p,
     out_table,
+    cell,
+    offset,
+    velocity,
+    affine,
+    mass,
+    dep,
+    parts,
+    load_sem,
     lin_row,
     lins,
     got,
@@ -196,6 +217,39 @@
     reply_recv,
 ):
     me = [lax.axis_index(name) for name in AXES]
+    bins = cell.shape[0]
+    chunks = [
+        (start, min(STEP_BINS, bins - start))
+        for start in [*range(SELF_BINS, bins, STEP_BINS), *range(0, SELF_BINS, STEP_BINS)]
+    ]
+    loads = []
+    for index, (start, rows) in enumerate(chunks):
+        span = pl.ds(start, rows)
+        sems = iter(range(5))
+        loads.append(
+            [
+                pltpu.make_async_copy(src.at[span], dst.at[span], load_sem.at[index, next(sems)])
+                for src, dst in ((cell_h, cell), (mass_h, mass))
+            ]
+            + [
+                pltpu.make_async_copy(
+                    src.at[:, span], dst.at[:, span], load_sem.at[index, next(sems)]
+                )
+                for src, dst in ((offset_h, offset), (velocity_h, velocity), (affine_h, affine))
+            ]
+        )
+        for load in loads[-1]:
+            load.start()
+
+    def splat(index):
+        for load in loads[index]:
+            load.wait()
+        start, rows = chunks[index]
+        splat_chunk(
+            start, rows, tpd, owner, tile, count, cell, offset, velocity, affine, mass, parts, dep
+        )
+
+    far_chunks = len(chunks) - SELF_BINS // STEP_BINS
 
     def inside(rel):
         ok = None
@@ -235,6 +289,8 @@
         1 + (me[n] > 0).astype(jnp.int32) + (me[n] < sizes[n] - 1).astype(jnp.int32)
         for n in range(3)
     ]
+    for index in range(far_chunks):
+        splat(index)
     pl.semaphore_wait(barrier, spans[0] * spans[1] * spans[2] - 1)
 
     def part_copy(number):
@@ -321,6 +377,8 @@
             part_copy(number).start()
 
     start_faces(lin_copy)
+    for index in range(far_chunks, len(chunks)):
+        splat(index)
 
     def hot_of(ref, rows):
         slots = ref[pl.ds(QROWS, rows, stride=BLOCK), :]
@@ -474,27 +532,9 @@
     by_component = [
         jnp.transpose(x, (1, 0, 2)) for x in (part_offset, part_velocity, part_affine)
     ]
-    parts = pl.pallas_call(
-        functools.partial(splat_kernel, bins, tpd),
-        out_shape=jax.ShapeDtypeStruct((bins * BLOCK, LANES), f32),
-        grid_spec=pltpu.PrefetchScalarGridSpec(
-            num_scalar_prefetch=3,
-            grid=(steps,),
-            in_specs=[
-                pl.BlockSpec((STEP_BINS, points), rows),
-                pl.BlockSpec((3, STEP_BINS, points), slabs),
-                pl.BlockSpec((3, STEP_BINS, points), slabs),
-                pl.BlockSpec((9, STEP_BINS, points), slabs),
-                pl.BlockSpec((STEP_BINS, points), rows),
-            ],
-            out_specs=pl.BlockSpec((STEP_BINS * BLOCK, LANES), rows),
-            scratch_shapes=[pltpu.VMEM((4, STEP_BINS, points), f32)],
-        ),
-        compiler_params=pltpu.CompilerParams(dimension_semantics=("arbitrary",)),
-        name="splat",
-    )(owner_map, bin_tile, bin_count, part_cell, *by_component, part_mass)
-
     vmem = pl.BlockSpec(memory_space=pltpu.VMEM)
+    smem = pl.BlockSpec(memory_space=pltpu.SMEM)
+    hbm = pl.BlockSpec(memory_space=pl.ANY)
     dma = pltpu.SemaphoreType.DMA
     count = len(OFFSETS)
     velocity, pressure, table = pl.pallas_call(
@@ -504,9 +544,17 @@
             jax.ShapeDtypeStruct((tpd * GROUPS, LANES), f32),
             jax.ShapeDtypeStruct(((tpd + near) * QROWS, LANES), f32),
         ),
-        in_specs=[vmem] * 2,
+        in_specs=[smem] * 3 + [vmem] + [hbm] * 5,
         out_specs=(vmem, vmem, vmem),
         scratch_shapes=[
+            pltpu.VMEM((bins, points), jnp.int32),
+            pltpu.VMEM((3, bins, points), f32),
+            pltpu.VMEM((3, bins, points), f32),
+            pltpu.VMEM((9, bins, points), f32),
+            pltpu.VMEM((bins, points), f32),
+            pltpu.VMEM((4, STEP_BINS, points), f32),
+            pltpu.VMEM((bins * BLOCK, LANES), f32),
+            dma((steps, 5)),
             pltpu.VMEM((8, LANES), f32),
             pltpu.VMEM((6, 8, LANES), f32),
             pltpu.VMEM((near_pad * BLOCK, LANES), f32),
@@ -525,7 +573,7 @@
         ],
         compiler_params=pltpu.CompilerParams(collective_id=0, has_side_effects=True),
         name="grid",
-    )(tile_coords, parts)
+    )(owner_map, bin_tile, bin_count, tile_coords, part_cell, *by_component, part_mass)
 
     sampled = pl.pallas_call(
         functools.partial(sample_kernel, bins, tpd),

time: 63.6 us -> 55.4 us (0.87)
  Pallas kernels: 61.4 us -> 53.3 us
    pallas_call x1 -> x0, Pallas kernels: 14.7 us -> none  [local(): pl.pallas_call(functools.partial(splat_kernel, bins, tpd), out_shape=jax....]
    pallas_call x1, Pallas kernels: 36.1 us -> 42.6 us  [local(): pl.pallas_call(functools.partial(grid_kernel, sizes, tpd, per, near_pad),...]
where the time goes in v4:
time: 55.4 us; the launch traced here: 55.2 us
  Pallas kernels  53.3 us (96%)
  local copies, waits for them, and re-layouts  1.28 us (2%)
  between operations  0.66 us (1%)
    pallas_call x1, Pallas kernels, local(): pl.pallas_call(functools.partial(grid_kernel, sizes, tpd, per, near_pad),...  42.6 us
    pallas_call x1, Pallas kernels, local(): pl.pallas_call(functools.partial(sample_kernel, bins, tpd), out_shape=jax...  10.6 us
    unnamed x6, local copies, waits for them, and re-layouts  1.28 us

profile of v4, /device:TPU:0, one launch (start us, length us, event | category | flops | bytes accessed | tf_op | source)
XLA Modules:
  0.0 55.2 jit_solution(2730142850307250146)
XLA Ops:
  0.6 42.6 %grid.1 = (f32[3,8192]{1,0:T(4,128)}, f32[64,128]{1,0:T(8,128)}, f32[672,128]{1,0:T(8,128)}) custom-call(s32[512]{0:T(512)} %owner.3, s32[58]{0:T(128)} %tile.3, s32[58]{0:T(128)} %count.3, s32[3,16]{1,0:T(4,128)} %coords.1, s32[58,2048]{1,0:T(8,128)} %cell.1, f32[3,58,2048]{2,1,0:T(8,128)} %bitcast.7, f32[3,58,2048]{2,1,0:T(8,128)} %bitcast.8, ...), custom_call_target="tpu_custom_call" | custom-call | tf_op jit(solution)/shard_map/grid/pallas_call | solution.py:540
  43.3 0.0 copy-start
  43.3 0.0 copy-start.1
  43.3 10.6 %sample.1 = f32[3,58,2048]{2,1,0:T(8,128)} custom-call(s32[512]{0:T(512)} %owner.3, s32[58]{0:T(128)} %tile.3, s32[58]{0:T(128)} %count.3, s32[58,2048]{1,0:T(8,128)} %cell.1, f32[672,128]{1,0:T(8,128)} %get-tuple-element.8.table), custom_call_target="tpu_custom_call" | custom-call | tf_op jit(solution)/shard_map/sample/pallas_call | solution.py:578
  54.0 0.0 copy-done
  54.0 0.7 %copy.14 = f32[3,8192]{1,0:T(4,128)} copy(f32[3,8192]{1,0:T(4,128)S(1)} %copy-done) | data formatting | bytes 196608
  54.6 0.0 copy-done.1
  54.6 0.6 %copy.15 = f32[8192]{0:T(1024)} copy(f32[8192]{0:T(1024)S(1)} %bitcast.9) | data formatting | bytes 65536
Async XLA Ops:
  43.3 10.7 %copy-start = (f32[3,8192]{1,0:T(4,128)S(1)}, f32[3,8192]{1,0:T(4,128)}, u32[]{:S(2)}) copy-start(f32[3,8192]{1,0:T(4,128)} %get-tuple-element.12) | copy-start | bytes 294916
  43.3 11.3 %copy-start.1 = (f32[64,128]{1,0:T(8,128)S(1)}, f32[64,128]{1,0:T(8,128)}, u32[]{:S(2)}) copy-start(f32[64,128]{1,0:T(8,128)} %get-tuple-element.7) | copy-start | bytes 98308

commit v5 on v4

--- a/solution.py
+++ b/solution.py
@@ -43,16 +43,30 @@
     return jnp.where(lane < count, cell_row >> 7, -1)
 
 
-def bins_of_step(step, bins, body):
-    left = jnp.minimum(STEP_BINS, bins - step * STEP_BINS)
-    unroll = 2 if bins % 2 == 0 else 1
-
-    def pair(i, carry):
+def unrolled(rows, body):
+    unroll = next(n for n in (4, 2, 1) if rows % n == 0)
+
+    def group(i, carry):
         for k in range(unroll):
             body(i * unroll + k)
         return carry
 
-    lax.fori_loop(0, left // unroll, pair, 0)
+    lax.fori_loop(0, rows // unroll, group, 0)
+
+
+def bins_of_step(step, bins, body):
+    tail = bins % STEP_BINS
+    full = bins // STEP_BINS
+
+    @pl.when(step < full)
+    def _():
+        unrolled(STEP_BINS, body)
+
+    if tail:
+
+        @pl.when(step == full)
+        def _():
+            unrolled(tail, body)
 
 
 def splat_chunk(start, rows, tpd, owner, tile, count, cell, offset, velocity, affine, mass, out, dep):
@@ -90,14 +104,7 @@
         slot = lax.rem(owner[tile[b]], tpd).astype(jnp.float32)
         out[pl.ds(base + QROWS, 8), :] = jnp.full((8, LANES), slot, jnp.float32)
 
-    unroll = 2 if rows % 2 == 0 else 1
-
-    def pair(i, carry):
-        for k in range(unroll):
-            one(i * unroll + k)
-        return carry
-
-    lax.fori_loop(0, rows // unroll, pair, 0)
+    unrolled(rows, one)
 
 
 def sample_kernel(bins, slots_of, owner, tile, count, cell, table, out):

time: 55.4 us -> 52.3 us (0.944)
  Pallas kernels: 53.3 us -> 49.8 us
    pallas_call x1, Pallas kernels: 42.6 us -> 40.9 us  [local(): pl.pallas_call(functools.partial(grid_kernel, sizes, tpd, per, near_pad),...]
    pallas_call x1, Pallas kernels: 10.6 us -> 8.98 us  [local(): pl.pallas_call(functools.partial(sample_kernel, bins, tpd), out_shape=jax...]
where the time goes in v5:
time: 52.3 us; the launch traced here: 51.8 us
  Pallas kernels  49.8 us (95%)
  local copies, waits for them, and re-layouts  1.28 us (2%)
  between operations  0.66 us (1%)
    pallas_call x1, Pallas kernels, local(): pl.pallas_call(functools.partial(grid_kernel, sizes, tpd, per, near_pad),...  40.9 us
    pallas_call x1, Pallas kernels, local(): pl.pallas_call(functools.partial(sample_kernel, bins, tpd), out_shape=jax...  8.98 us
    unnamed x6, local copies, waits for them, and re-layouts  1.28 us

profile of v5, /device:TPU:0, one launch (start us, length us, event | category | flops | bytes accessed | tf_op | source)
XLA Modules:
  0.0 51.8 jit_solution(16384750696388204972)
XLA Ops:
  0.6 40.9 %grid.1 = (f32[3,8192]{1,0:T(4,128)}, f32[64,128]{1,0:T(8,128)}, f32[672,128]{1,0:T(8,128)}) custom-call(s32[512]{0:T(512)} %owner.3, s32[58]{0:T(128)} %tile.3, s32[58]{0:T(128)} %count.3, s32[3,16]{1,0:T(4,128)} %coords.1, s32[58,2048]{1,0:T(8,128)} %cell.1, f32[3,58,2048]{2,1,0:T(8,128)} %bitcast.7, f32[3,58,2048]{2,1,0:T(8,128)} %bitcast.8, ...), custom_call_target="tpu_custom_call" | custom-call | tf_op jit(solution)/shard_map/grid/pallas_call | solution.py:547
  41.5 0.0 copy-start
  41.5 0.0 copy-start.1
  41.5 9.0 %sample.1 = f32[3,58,2048]{2,1,0:T(8,128)} custom-call(s32[512]{0:T(512)} %owner.3, s32[58]{0:T(128)} %tile.3, s32[58]{0:T(128)} %count.3, s32[58,2048]{1,0:T(8,128)} %cell.1, f32[672,128]{1,0:T(8,128)} %get-tuple-element.8.table), custom_call_target="tpu_custom_call" | custom-call | tf_op jit(solution)/shard_map/sample/pallas_call | solution.py:585
  50.5 0.0 copy-done
  50.5 0.7 %copy.14 = f32[3,8192]{1,0:T(4,128)} copy(f32[3,8192]{1,0:T(4,128)S(1)} %copy-done) | data formatting | bytes 196608
  51.2 0.0 copy-done.1
  51.2 0.6 %copy.15 = f32[8192]{0:T(1024)} copy(f32[8192]{0:T(1024)S(1)} %bitcast.9) | data formatting | bytes 65536
Async XLA Ops:
  41.5 9.0 %copy-start = (f32[3,8192]{1,0:T(4,128)S(1)}, f32[3,8192]{1,0:T(4,128)}, u32[]{:S(2)}) copy-start(f32[3,8192]{1,0:T(4,128)} %get-tuple-element.12) | copy-start | bytes 294916
  41.5 9.6 %copy-start.1 = (f32[64,128]{1,0:T(8,128)S(1)}, f32[64,128]{1,0:T(8,128)}, u32[]{:S(2)}) copy-start(f32[64,128]{1,0:T(8,128)} %get-tuple-element.7) | copy-start | bytes 98308
